TPU v7x, 128 devices: a whole 4x4x4 slice. The times are simulated.
128 devices in a mesh: row: 16 (over x, z_lo, core), col: 8 (over y, z_hi).
Axes of the slice: x: 4, y: 4, z: 4 (z_hi: 2, z_lo: 2; z = z_hi * 2 + z_lo), core: 2. Of those that a mesh axis runs over, the one named last changes fastest.
Arguments:
- entities: bfloat16 [2, 131072, 200], P(None, ('row', 'col')), may hold values from -2.390625 to 2.390625
- relations: bfloat16 [2, 1024, 200], replicated, may hold values from -6 to 6
- src_index: int32 [524288], P(('row', 'col')), may hold values from 0 to 8191
- dst_index: int32 [524288], P(('row', 'col')), may hold values from 0 to 16383
- rel_index: int32 [524288], P(('row', 'col')), may hold values from 0 to 1023
- neg_block: int32 [1024], P(('row', 'col')), may hold values from 0 to 31
Outputs:
- edge_loss: float32 [524288], P(('row', 'col'))
- relation_grad: float32 [2, 1024, 200], P(None, ('row', 'col'))
All inputs are finite; a program needn't handle non-finite values.
Results may differ from a plain program's by a relative error of at most 0.0018.
Values may be sent and summed in bfloat16 or wider, within the bound.
No kernel may reach another device: no remote copies, remote signals or barrier semaphores. Data moves between devices by JAX's collectives and lax.ppermute only.
A program may use at most 128 MiB of HBM per device.

v0:
```python
import jax
import jax.numpy as jnp
from jax import lax
from jax.sharding import PartitionSpec as P

NEGB = 512


def cut_along(array, dim, count):
    lengths = array.shape
    parts = array.reshape(*lengths[:dim], count, lengths[dim] // count, *lengths[dim + 1 :])
    return jnp.moveaxis(parts, dim, 0)


def sum_at_owner(array, axis, dim):
    count = lax.axis_size(axis)
    parts = lax.all_to_all(cut_along(array, dim, count), axis, 0, 0, tiled=True)
    return jnp.sum(parts, axis=0)


def bucket_terms(picked_src, picked_dst, negatives, relations, rel_ids):
    onehot = (rel_ids[:, None] == jnp.arange(relations.shape[1], dtype=jnp.int32)[None, :]).astype(
        jnp.bfloat16
    )
    rel_re = jnp.dot(onehot, relations[0], preferred_element_type=jnp.float32)
    rel_im = jnp.dot(onehot, relations[1], preferred_element_type=jnp.float32)
    src_re = picked_src[0].astype(jnp.float32)
    src_im = picked_src[1].astype(jnp.float32)
    dst_re = picked_dst[0].astype(jnp.float32)
    dst_im = picked_dst[1].astype(jnp.float32)
    query_re = src_re * rel_re - src_im * rel_im
    query_im = src_re * rel_im + src_im * rel_re
    pos_score = jnp.sum(query_re * dst_re, 1) + jnp.sum(query_im * dst_im, 1)
    groups = negatives.shape[1]
    dim = query_re.shape[1]
    qre_b = query_re.astype(jnp.bfloat16).reshape(groups, -1, dim)
    qim_b = query_im.astype(jnp.bfloat16).reshape(groups, -1, dim)
    neg_score = jnp.einsum(
        "kcd,knd->kcn", qre_b, negatives[0], preferred_element_type=jnp.float32
    ) + jnp.einsum("kcd,knd->kcn", qim_b, negatives[1], preferred_element_type=jnp.float32)
    edge_loss = jax.nn.softplus(-pos_score) + jnp.mean(jax.nn.softplus(neg_score), -1).reshape(-1)
    weights = (jax.nn.sigmoid(neg_score) / NEGB).astype(jnp.bfloat16)
    gneg_re = jnp.einsum(
        "kcn,knd->kcd", weights, negatives[0], preferred_element_type=jnp.float32
    ).reshape(-1, dim)
    gneg_im = jnp.einsum(
        "kcn,knd->kcd", weights, negatives[1], preferred_element_type=jnp.float32
    ).reshape(-1, dim)
    pull = jax.nn.sigmoid(-pos_score)[:, None]
    grad_re = gneg_re - pull * dst_re
    grad_im = gneg_im - pull * dst_im
    term_re = (grad_re * src_re + grad_im * src_im).astype(jnp.bfloat16)
    term_im = (grad_im * src_re - grad_re * src_im).astype(jnp.bfloat16)
    dims = (((0,), (0,)), ((), ()))
    rel_grad = jnp.stack(
        [
            lax.dot_general(onehot, term_re, dims, preferred_element_type=jnp.float32),
            lax.dot_general(onehot, term_im, dims, preferred_element_type=jnp.float32),
        ],
        0,
    )
    return (edge_loss, rel_grad)


def body(entities, relations, src_index, dst_index, rel_index, neg_block):
    dim = entities.shape[2]
    source_rows = lax.all_gather(entities, "col", axis=1, tiled=True)
    picked_src = jnp.take(source_rows, src_index, axis=1)
    target_rows = lax.all_gather(entities, "row", axis=1, tiled=True)
    picked_dst = jnp.take(target_rows, dst_index, axis=1)
    negatives = jnp.take(target_rows.reshape(2, -1, NEGB, dim), neg_block, axis=1)
    edge_loss, rel_grad = bucket_terms(picked_src, picked_dst, negatives, relations, rel_index)
    row_share = sum_at_owner(rel_grad, "row", 1)
    grad_share = sum_at_owner(row_share, "col", 1)
    return (edge_loss, grad_share)


def solution(mesh):
    placed = (
        P(None, ("row", "col"), None),
        P(),
        P(("row", "col")),
        P(("row", "col")),
        P(("row", "col")),
        P(("row", "col")),
    )
    return jax.shard_map(
        body,
        mesh=mesh,
        in_specs=placed,
        out_specs=(P(("row", "col")), P(None, ("row", "col"), None)),
        check_vma=False,
    )
```

profile of v0, /device:TPU:0, one launch (start us, length us, event | category | flops | bytes accessed | tf_op | source)
XLA Modules:
  0.0 415.5 jit_solution(14497908831256635601)
XLA Ops:
  12.9 6.4 %fusion.4 = f32[4096,200]{0,1:T(8,128)} fusion(s32[4096]{0:T(1024)} %param.10, bf16[2,1024,200]{1,2,0:T(8,128)(2,1)} %param.7), kind=kOutput, calls=%fused_computation.8 | convolution fusion | flops 1681915904 | bytes 3702784 | tf_op jit(solution)/shard_map/dot_general | solution.py:26
  19.2 85.7 %all-gather.3.cloned.1.call-done = bf16[2,8192,200]{1,2,0:T(8,128)(2,1)} async-done(((bf16[2,1024,200]{1,2,0:T(8,128)(2,1)}), bf16[2,8192,200]{1,2,0:T(8,128)(2,1)}) %all-gather.3.cloned.1.call-update) | async-done | bytes 6553616 | tf_op jit(solution)/shard_map/all_gather | solution.py:67
  104.9 21.0 %copy.54 = bf16[2,8192,200]{2,0,1:T(2,128)(2,1)} copy(bf16[2,8192,200]{1,2,0:T(8,128)(2,1)} %all-gather.3.cloned.1.call-done) | data formatting | bytes 13107200 | tf_op jit(solution)/shard_map/all_gather | solution.py:67
  125.9 36.0 %gather_fusion = bf16[4096,2,200]{2,1,0:T(2,128)(2,1)} fusion(bf16[2,8192,200]{2,0,1:T(2,128)(2,1)} %copy.54, s32[4096]{0:T(1024)S(1)} %fusion.36), kind=kCustom, calls=%fused_computation | custom fusion | bytes 6569984 | tf_op jit(solution)/shard_map/jit(_take)/gather | solution.py:68
  161.9 9.3 %copy.55 = bf16[4096,2,200]{0,2,1:T(8,128)(2,1)S(1)} copy(bf16[4096,2,200]{2,1,0:T(2,128)(2,1)} %gather_fusion) | data formatting | bytes 6553600 | tf_op jit(solution)/shard_map/jit(_take)/gather | solution.py:68
  171.2 7.5 %all-gather.5.cloned.1.call-done = bf16[2,16384,200]{1,2,0:T(8,128)(2,1)} async-done(((bf16[2,1024,200]{1,2,0:T(8,128)(2,1)}), bf16[2,16384,200]{1,2,0:T(8,128)(2,1)}) %all-gather.5.cloned.1.call-update) | async-done | bytes 13107216 | tf_op jit(solution)/shard_map/all_gather | solution.py:69
  178.7 40.3 %copy.56 = bf16[2,16384,200]{2,0,1:T(2,128)(2,1)} copy(bf16[2,16384,200]{1,2,0:T(8,128)(2,1)} %all-gather.5.cloned.1.call-done) | data formatting | bytes 26214400 | tf_op jit(solution)/shard_map/all_gather | solution.py:69
  219.0 38.2 %gather_fusion.1 = bf16[4096,2,200]{2,1,0:T(2,128)(2,1)} fusion(bf16[2,16384,200]{2,0,1:T(2,128)(2,1)} %copy.56, s32[4096]{0:T(1024)S(1)} %fusion.37), kind=kCustom, calls=%fused_computation.1 | custom fusion | bytes 6569984 | tf_op jit(solution)/shard_map/jit(_take)/gather | solution.py:70
  257.3 11.0 %copy.57 = bf16[4096,2,200]{0,2,1:T(8,128)(2,1)} copy(bf16[4096,2,200]{2,1,0:T(2,128)(2,1)} %gather_fusion.1) | data formatting | bytes 6553600 | tf_op jit(solution)/shard_map/jit(_take)/gather | solution.py:70
  270.9 3.5 slice_convert_fusion
  274.4 4.1 slice_convert_fusion.3
  278.6 6.9 %fusion.12 = (f32[4096]{0:T(1024)S(1)}, f32[4096]{0:T(1024)S(1)}, bf16[4096,200]{0,1:T(8,128)(2,1)}, bf16[4096,200]{0,1:T(8,128)(2,1)}) fusion(bf16[2,4096,200]{1,2,0:T(8,128)(2,1)S(1)} %get-tuple-element.16, bf16[2,4096,200]{1,2,0:T(8,128)(2,1)S(1)} %get-tuple-element.17, f32[4096,200]{0,1:T(8,128)S(1)} %copy-done.12, ...), kind=kOutput, calls=%fused_computation.22 | convolution fusion | flops 1695014912 | bytes 13565952 | tf_op jit(solution)/shard_map/dot_general | solution.py:25
  285.5 5.4 %copy.108 = bf16[2,25,32,8,512]{4,3,1,2,0:T(8,128)(2,1)} copy(bf16[2,25,32,8,512]{4,3,2,1,0:T(8,128)(2,1)S(1)} %bitcast.118) | data formatting | bytes 26214400 | tf_op jit(solution)/shard_map/reshape | solution.py:71
  290.9 5.5 %gather_fusion.2 = bf16[8,2,512,200]{2,3,1,0:T(8,128)(2,1)S(1)} fusion(bf16[2,32,512,200]{2,3,1,0:T(8,128)(2,1)} %bitcast.121, s32[1024]{0:T(1024)S(1)} %pad_clamp_fusion), kind=kCustom, calls=%fused_computation.2 | custom fusion | bytes 6553632 | tf_op jit(solution)/shard_map/jit(_take)/gather | solution.py:71
  302.0 5.2 %select_reduce_fusion = f32[8,512]{1,0:T(8,128)S(1)} fusion(f32[8,512,512]{1,2,0:T(8,128)S(1)} %get-tuple-element.15, u8[512,512]{0,1:T(8,128)(4,1)S(1)} %get-tuple-element.14), kind=kLoop, calls=%fused_computation.18 | loop fusion | flops 20967424 | bytes 8667136 | tf_op jit(solution)/shard_map/reduce_sum | solution.py:41
  308.0 4.7 %copy.80 = f32[25,8,8,512]{3,2,1,0:T(8,128)} copy(f32[25,8,8,512]{3,1,2,0:T(8,128)S(1)} %bitcast.124) | data formatting | bytes 6553600
  312.7 2.9 copy.81
  315.7 2.9 copy.82
  318.6 14.5 %copy.83 = f32[25,8,8,512]{3,2,1,0:T(8,128)} copy(f32[25,8,8,512]{3,1,2,0:T(8,128)S(1)} %bitcast.123) | data formatting | bytes 6553600
  333.1 6.1 %fusion.17 = f32[8,512,200]{1,2,0:T(8,128)} fusion(f32[8,512,200]{1,0,2:T(8,128)} %bitcast.129, f32[8,512]{1,0:T(8,128)S(1)} %div.35, bf16[2,8,512,200]{2,3,1,0:T(8,128)(2,1)S(1)} %copy-done.6, f32[8,512,512]{1,2,0:T(8,128)S(1)} %bitcast.120), kind=kOutput, calls=%fused_computation.34 | convolution fusion | flops 850984960 | bytes 16596992 | tf_op jit(solution)/shard_map/kcn,knd->kcd/dot_general | solution.py:43
  339.3 9.7 %add_convert_fusion = (bf16[8,512,200]{1,2,0:T(8,128)(2,1)}, bf16[8,512,200]{1,2,0:T(8,128)(2,1)}) fusion(f32[8,512,200]{1,2,0:T(8,128)} %fusion.17, f32[8,512,200]{1,0,2:T(8,128)} %bitcast.128, f32[8,512,200]{1,0,2:T(8,128)S(1)} %bitcast.126, f32[8,512,200]{1,0,2:T(8,128)S(1)} %bitcast.127, f32[8,512]{1,0:T(8,128)S(1)} %div.35, ...), kind=kOutput, calls=%fused_computation.40 | convolution fusion | flops 857538560 | bytes 26427392 | tf_op jit(solution)/shard_map/kcn,knd->kcd/dot_general | solution.py:46
  354.2 3.9 fusion.25
  360.9 32.5 %all_to_all.10 = f32[16,2,64,200]{3,2,1,0:T(8,128)S(1)} all-to-all(f32[16,2,64,200]{3,2,1,0:T(8,128)S(1)} %copy.72), channel_id=1, replica_groups=mesh['row'=16,'col'=8] {'row'}, dimensions={0} | all-to-all | bytes 3276800 | tf_op jit(solution)/shard_map/all_to_all | solution.py:17
  393.6 14.3 %all_to_all.11 = f32[8,2,8,200]{3,2,1,0:T(8,128)S(1)} all-to-all(f32[8,2,8,200]{3,2,1,0:T(8,128)S(1)} %copy.73), channel_id=1, replica_groups=mesh['row'=16,'col'=8] {'col'}, dimensions={0} | all-to-all | bytes 204800 | tf_op jit(solution)/shard_map/all_to_all | solution.py:17
  (70 shorter events, 23.4 us)
Async XLA Ops:
  7.2 97.8 %all-gather.3.cloned.1.call-start = ((), (), s32[]{:S(2)}) async-start(), calls=%async_computation.2 | async-start | bytes 7372800 | tf_op jit(solution)/shard_map/all_gather | solution.py:67
  7.9 170.8 %all-gather.5.cloned.1.call-start = ((), (), s32[]{:S(2)}) async-start(), calls=%async_computation.3 | async-start | bytes 13926400 | tf_op jit(solution)/shard_map/all_gather | solution.py:69
  274.4 4.2 copy-start.10
  274.4 4.2 %copy-start.11 = (s32[4096]{0:T(1024)S(1)}, s32[4096]{0:T(1024)}, u32[]{:S(2)}) copy-start(s32[4096]{0:T(1024)} %param.10) | copy-start | bytes 49156
  274.4 4.2 %copy-start.12 = (f32[4096,200]{0,1:T(8,128)S(1)}, f32[4096,200]{0,1:T(8,128)}, u32[]{:S(2)}) copy-start(f32[4096,200]{0,1:T(8,128)} %fusion.4) | copy-start | bytes 9830404
  274.4 11.0 %slice-start = ((s8[13107200]{0:T(1024)(128)(4,1)}), s8[4194304]{0:T(1024)(128)(4,1)S(1)}, s32[]{:S(2)}) async-start(s8[13107200]{0:T(1024)(128)(4,1)} %bitcast.116), calls=%async_computation.4 | async-start | bytes 8388608
  274.4 11.0 %slice-start.1 = ((s8[13107200]{0:T(1024)(128)(4,1)}), s8[524288]{0:T(1024)(128)(4,1)S(1)}, s32[]{:S(2)}) async-start(s8[13107200]{0:T(1024)(128)(4,1)} %bitcast.116), calls=%async_computation.5 | async-start | bytes 1048576
  278.6 6.9 %slice-start.2 = ((s8[13107200]{0:T(1024)(128)(4,1)}), s8[4194304]{0:T(1024)(128)(4,1)S(1)}, s32[]{:S(2)}) async-start(s8[13107200]{0:T(1024)(128)(4,1)} %bitcast.116), calls=%async_computation.6 | async-start | bytes 8388608
  278.6 6.9 %slice-start.3 = ((s8[13107200]{0:T(1024)(128)(4,1)}), s8[4194304]{0:T(1024)(128)(4,1)S(1)}, s32[]{:S(2)}) async-start(s8[13107200]{0:T(1024)(128)(4,1)} %bitcast.116), calls=%async_computation.7 | async-start | bytes 8388608
  296.4 1.6 copy-start.9
  296.8 2.6 copy-start.5
  298.0 1.4 copy-start.7
  302.0 5.3 %copy-start = (f32[8,512,512]{1,2,0:T(8,128)}, f32[8,512,512]{1,2,0:T(8,128)S(1)}, u32[]{:S(2)}) copy-start(f32[8,512,512]{1,2,0:T(8,128)S(1)} %get-tuple-element.15) | copy-start | bytes 25165828
  302.0 5.9 %copy-start.3 = (f32[1,4096,200]{1,2,0:T(8,128)S(1)}, f32[1,4096,200]{1,2,0:T(8,128)}, u32[]{:S(2)}) copy-start(f32[1,4096,200]{1,2,0:T(8,128)} %get-tuple-element.11) | copy-start | bytes 9830404
  308.0 4.7 %copy-start.4 = (f32[1,4096,200]{1,2,0:T(8,128)S(1)}, f32[1,4096,200]{1,2,0:T(8,128)}, u32[]{:S(2)}) copy-start(f32[1,4096,200]{1,2,0:T(8,128)} %get-tuple-element.8) | copy-start | bytes 9830404
  308.0 7.7 %copy-start.1 = (f32[1,4096,200]{1,2,0:T(8,128)S(1)}, f32[1,4096,200]{1,2,0:T(8,128)}, u32[]{:S(2)}) copy-start(f32[1,4096,200]{1,2,0:T(8,128)} %get-tuple-element.10) | copy-start | bytes 9830404
  312.7 5.9 %copy-start.2 = (f32[1,4096,200]{1,2,0:T(8,128)S(1)}, f32[1,4096,200]{1,2,0:T(8,128)}, u32[]{:S(2)}) copy-start(f32[1,4096,200]{1,2,0:T(8,128)} %get-tuple-element.9) | copy-start | bytes 9830404
  312.7 20.4 %slice-start.4 = ((s8[8388608]{0:T(1024)(128)(4,1)}), s8[4194304]{0:T(1024)(128)(4,1)S(1)}, s32[]{:S(2)}) async-start(s8[8388608]{0:T(1024)(128)(4,1)} %bitcast.119), calls=%async_computation.8 | async-start | bytes 8388608
  315.7 17.5 %slice-start.5 = ((s8[8388608]{0:T(1024)(128)(4,1)}), s8[4194304]{0:T(1024)(128)(4,1)S(1)}, s32[]{:S(2)}) async-start(s8[8388608]{0:T(1024)(128)(4,1)} %bitcast.119), calls=%async_computation.9 | async-start | bytes 8388608
  318.6 14.5 %copy-start.6 = (bf16[2,8,512,200]{2,3,1,0:T(8,128)(2,1)S(1)}, bf16[2,8,512,200]{2,3,1,0:T(8,128)(2,1)}, u32[]{:S(2)}) copy-start(bf16[2,8,512,200]{2,3,1,0:T(8,128)(2,1)} %copy-done.5) | copy-start | bytes 9830404
  348.9 4.0 copy-start.8
Sparse Core Ops, SparseCore 0:
  10.4 94.5 all-gather.2
  106.6 72.0 all-gather.4
where the time goes:
time: 422 us; the launch traced here: 415 us
  local copies, waits for them, and re-layouts  199 us (47%)
  waiting for transfers between devices  94.6 us (22%)
  blocking collectives  46.8 us (11%)
  matrix products  39.3 us (9%)
  other arithmetic  21.7 us (5%)
  between operations  14.5 us (3%)
    all_gather x1, waiting for transfers between devices, body(): source_rows = lax.all_gather(entities, 'col', axis=1, tiled=True)  85.7 us
    gather x2, local copies, waits for them, and re-layouts, body(): picked_dst = jnp.take(target_rows, dst_index, axis=1)  49.2 us
    all_to_all x2, blocking collectives, sum_at_owner(): parts = lax.all_to_all(cut_along(array, dim, count), axis, 0, 0, tiled=True)  46.8 us
    gather x2, local copies, waits for them, and re-layouts, body(): picked_src = jnp.take(source_rows, src_index, axis=1)  45.2 us
    all_gather x1, local copies, waits for them, and re-layouts, body(): target_rows = lax.all_gather(entities, 'row', axis=1, tiled=True)  40.3 us
    unnamed x43, local copies, waits for them, and re-layouts  26.4 us
    all_gather x1, local copies, waits for them, and re-layouts, body(): source_rows = lax.all_gather(entities, 'col', axis=1, tiled=True)  21 us
    dot_general x1, matrix products, bucket_terms(): jnp.einsum('kcn,knd->kcd', weights, negatives[1], preferred_element_type=...  9.68 us
  transfers between devices with their start and end apart: 2, of which 2 were waited for; matrix products, arithmetic and copies ran while one was open for 18% of the time, Pallas kernels for 0%

commit v1 on v0

v1 whole, which is shorter than its diff:
```python
import functools

import jax
import jax.numpy as jnp
from jax import lax
from jax.experimental import pallas as pl
from jax.experimental.pallas import tpu as pltpu
from jax.sharding import PartitionSpec as P

F32, BF16 = jnp.float32, jnp.bfloat16
SHARD = 1024
EDGES = 4096
GROUP = 512
NEGB = 512
HALF = 256
WIDE = 2 * HALF
DIM = 200
NREL = 1024
STEPS = EDGES // GROUP
BOTH = ("row", "col")


def hop(array, dy=0, flip=0):
    pairs = []
    for r in range(16):
        for c in range(8):
            y, h = c // 2, c % 2
            pairs.append((r * 8 + c, r * 8 + ((y + dy) % 4) * 2 + (h ^ flip)))
    return lax.ppermute(array, BOTH, pairs)


def column_shards(own):
    pair = hop(own, flip=1)
    up, down = hop(own, dy=1), hop(own, dy=-1)
    pair_up, pair_down = hop(pair, dy=1), hop(pair, dy=-1)
    up2, pair_down2 = hop(up, dy=1), hop(pair_down, dy=-1)
    c = lax.axis_index("col")
    y, h = c // 2, c % 2
    at = lambda dy, flip: ((y - dy) % 4) * 2 + (h ^ flip)
    order = jnp.stack([at(0, 0), at(0, 1), at(1, 0), at(-1, 0), at(1, 1), at(-1, 1), at(2, 0), at(-2, 1)])
    return [own, pair, up, down, pair_up, pair_down, up2, pair_down2], order.astype(jnp.int32)


def fill_rows(columns, start, table):
    def tile(t, carry):
        n = pl.multiple_of(t * 128, 128)
        for part in range(2):
            head = columns[part, 0:128, pl.ds(n, 128)].astype(F32)
            tail = columns[part, 128:DIM, pl.ds(n, 128)].astype(F32)
            tail = jnp.concatenate([tail, jnp.zeros((HALF - DIM, 128), F32)], 0)
            table[pl.ds(start + n, 128), 2 * part, :] = head.T
            table[pl.ds(start + n, 128), 2 * part + 1, :] = tail.T
        return carry

    lax.fori_loop(0, SHARD // 128, tile, 0)


def pick_rows(index, first, table, rows, unroll=16):
    def step(i, carry):
        b = i * unroll
        values = [table[index[first + b + u]] for u in range(unroll)]
        for u in range(unroll):
            rows[b + u] = values[u]
        return carry

    lax.fori_loop(0, GROUP // unroll, step, 0)


def gather_kernel(count, index, order, *refs):
    shards, out = refs[:count], refs[count]
    held, table, rows, sem = refs[count + 1 :]
    g = pl.program_id(0)

    @pl.when(g == 0)
    def _():
        copies = [pltpu.make_async_copy(shards[j], held.at[j], sem.at[j]) for j in range(count)]
        for copy in copies:
            copy.start()
        for j in range(count):
            copies[j].wait()
            fill_rows(held.at[j], pl.multiple_of(order[j] * SHARD, SHARD), table)

    pick_rows(index, g * GROUP, table, rows)
    for k in range(4):
        out[:, k * 128 : (k + 1) * 128] = rows[:, k, :].astype(BF16)


def gather_rows(shards, order, index):
    count = len(shards)
    return pl.pallas_call(
        functools.partial(gather_kernel, count),
        out_shape=jax.ShapeDtypeStruct((EDGES, WIDE), BF16),
        grid_spec=pltpu.PrefetchScalarGridSpec(
            num_scalar_prefetch=2,
            grid=(STEPS,),
            in_specs=[pl.BlockSpec(memory_space=pl.ANY)] * count,
            out_specs=pl.BlockSpec((GROUP, WIDE), lambda g, *_: (g, 0)),
            scratch_shapes=[
                pltpu.VMEM((count, 2, DIM, SHARD), BF16),
                pltpu.VMEM((count * SHARD, 4, 128), F32),
                pltpu.VMEM((GROUP, 4, 128), F32),
                pltpu.SemaphoreType.DMA((count,)),
            ],
        ),
        compiler_params=pltpu.CompilerParams(vmem_limit_bytes=(8 + 4 * count) << 20),
        cost_estimate=pl.CostEstimate(flops=0, bytes_accessed=(5 + 2 * count) * 4_000_000, transcendentals=0),
        name="gather_rows",
    )(index, order, *shards)


BLOCK = 128


def group_kernel(index, blocks, target, src, rel, rel_ids, loss, grad, held, table, rows, negs, terms, sem):
    g = pl.program_id(0)

    @pl.when(g == 0)
    def _():
        copies = [pltpu.make_async_copy(target.at[j], held.at[j], sem.at[j]) for j in range(16)]
        for copy in copies:
            copy.start()
        negs[...] = jnp.zeros_like(negs)
        grad[...] = jnp.zeros_like(grad)
        for j in range(16):
            copies[j].wait()
            fill_rows(held.at[j], j * SHARD, table)

    pick_rows(index, g * GROUP, table, rows)
    block = blocks[g]
    half = pl.multiple_of((block % 2) * NEGB, NEGB)
    for part in range(2):
        negs[part * HALF : part * HALF + DIM, :] = held[block // 2, part, :, pl.ds(half, NEGB)]

    def piece(i, carry):
        at = pl.ds(pl.multiple_of(i * BLOCK, BLOCK), BLOCK)
        s = [src[at, k * 128 : (k + 1) * 128].astype(F32) for k in range(4)]
        w = [rel[at, k * 128 : (k + 1) * 128].astype(F32) for k in range(4)]
        o = [rows[at, k, :] for k in range(4)]
        q = [s[0] * w[0] - s[2] * w[2], s[1] * w[1] - s[3] * w[3], s[0] * w[2] + s[2] * w[0], s[1] * w[3] + s[3] * w[1]]
        pos = jnp.sum((q[0] * o[0] + q[1] * o[1]) + (q[2] * o[2] + q[3] * o[3]), axis=1, keepdims=True)
        qb = jnp.concatenate([v.astype(BF16) for v in q], axis=1)
        score = lax.dot_general(qb, negs[...], (((1,), (0,)), ((), ())), preferred_element_type=F32)
        low = jnp.exp(-jnp.abs(score))
        up = 1.0 + low
        weight = (jnp.where(score >= 0, 1.0 / NEGB, low * (1.0 / NEGB)) / up).astype(BF16)
        peak = jnp.maximum(score, 0.0)
        excess, total = low[:, 0:128], peak[:, 0:128]
        for k in range(1, 4):
            cut = slice(k * 128, (k + 1) * 128)
            excess = excess * up[:, cut] + low[:, cut]
            total = total + peak[:, cut]
        pull_low = jnp.exp(-jnp.abs(pos))
        pull = jnp.where(pos >= 0, pull_low, 1.0) / (1.0 + pull_low)
        pos_loss = jnp.maximum(-pos, 0.0) + jnp.log1p(pull_low)
        loss_part = (total + jnp.log1p(excess)) * (1.0 / NEGB) + pos_loss * (1.0 / 128)
        loss[0, :, at] = lax.dot_general(
            jnp.ones((8, 128), F32), loss_part, (((1,), (1,)), ((), ())),
            precision=lax.Precision.HIGHEST, preferred_element_type=F32,
        )[0:1]
        gneg = lax.dot_general(weight, negs[...], (((1,), (1,)), ((), ())), preferred_element_type=F32)
        d = [gneg[:, k * 128 : (k + 1) * 128] - pull * o[k] for k in range(4)]
        term = [d[0] * s[0] + d[2] * s[2], d[1] * s[1] + d[3] * s[3], d[2] * s[0] - d[0] * s[2], d[3] * s[1] - d[1] * s[3]]
        for k in range(4):
            terms[at, k * 128 : (k + 1) * 128] = term[k].astype(BF16)
        return carry

    for i in range(GROUP // BLOCK):
        piece(i, 0)
    ids = rel_ids[0]

    def scatter(i, carry):
        at = pl.ds(pl.multiple_of(i * 256, 256), 256)
        hot = (lax.broadcasted_iota(jnp.int32, (256, GROUP), 0) + i * 256) == ids
        hot = jnp.where(hot, 1.0, 0.0).astype(BF16)
        grad[at, :] += jnp.dot(hot, terms[...], preferred_element_type=F32)
        return carry

    lax.fori_loop(0, NREL // 256, scatter, 0)


def score_groups(target, dst_index, neg_block, src, rel, rel_index):
    return pl.pallas_call(
        group_kernel,
        out_shape=(jax.ShapeDtypeStruct((STEPS, 1, GROUP), F32), jax.ShapeDtypeStruct((NREL, WIDE), F32)),
        grid_spec=pltpu.PrefetchScalarGridSpec(
            num_scalar_prefetch=2,
            grid=(STEPS,),
            in_specs=[
                pl.BlockSpec(memory_space=pl.ANY),
                pl.BlockSpec((GROUP, WIDE), lambda g, *_: (g, 0)),
                pl.BlockSpec((GROUP, WIDE), lambda g, *_: (g, 0)),
                pl.BlockSpec((1, 1, GROUP), lambda g, *_: (g, 0, 0)),
            ],
            out_specs=[
                pl.BlockSpec((1, 1, GROUP), lambda g, *_: (g, 0, 0)),
                pl.BlockSpec((NREL, WIDE), lambda g, *_: (0, 0)),
            ],
            scratch_shapes=[
                pltpu.VMEM((16, 2, DIM, SHARD), BF16),
                pltpu.VMEM((16 * SHARD, 4, 128), F32),
                pltpu.VMEM((GROUP, 4, 128), F32),
                pltpu.VMEM((WIDE, NEGB), BF16),
                pltpu.VMEM((GROUP, WIDE), BF16),
                pltpu.SemaphoreType.DMA((16,)),
            ],
        ),
        compiler_params=pltpu.CompilerParams(vmem_limit_bytes=60 << 20),
        cost_estimate=pl.CostEstimate(flops=20_000_000_000, bytes_accessed=24_000_000, transcendentals=4_000_000),
        name="score_groups",
    )(dst_index, neg_block, target, src, rel, rel_index.reshape(STEPS, 1, GROUP))


def body(entities, relations, src_index, dst_index, rel_index, neg_block):
    own = jnp.swapaxes(entities, 1, 2)
    target = lax.all_gather(own, "row", axis=0)
    rel = gather_rows([jnp.swapaxes(relations, 1, 2)], jnp.zeros((1,), jnp.int32), rel_index)
    shards, order = column_shards(own)
    src = gather_rows(shards, order, src_index)
    loss, grad = score_groups(target, dst_index, neg_block, src, rel, rel_index)
    parts = lax.all_to_all(grad.reshape(128, 8, WIDE), BOTH, 0, 0, tiled=True)
    share = jnp.sum(parts, axis=0)
    share = jnp.stack([share[:, :DIM], share[:, HALF : HALF + DIM]])
    return loss.reshape(EDGES), share


def solution(mesh):
    placed = (
        P(None, BOTH, None),
        P(),
        P(BOTH),
        P(BOTH),
        P(BOTH),
        P(BOTH),
    )
    return jax.shard_map(
        body,
        mesh=mesh,
        in_specs=placed,
        out_specs=(P(BOTH), P(None, BOTH, None)),
        check_vma=False,
    )
```

time: 422 us -> 244 us (0.58); the launches traced: 415 us -> 242 us
  local copies, waits for them, and re-layouts: 199 us -> 5.86 us
  Pallas kernels: 0 us -> 117 us
  waiting for transfers between devices: 94.6 us -> 49.6 us
  matrix products: 39.3 us -> 0 us
  other arithmetic: 21.7 us -> 0.8 us
  starting transfers between devices: 0.08 us -> 14.4 us
  blocking collectives: 46.8 us -> 40.4 us
    pallas_call x0 -> x3, Pallas kernels: none -> 117 us  [the longest x1 71.2 us: score_groups(): pl.pallas_call(group_kernel, out_shape=(jax.ShapeDtypeStruct((STEPS, 1, G...]
    gather x5 -> x0, local copies, waits for them, and re-layouts: 100 us -> none  [the longest x2 49.2 us: body(): picked_dst = jnp.take(target_rows, dst_index, axis=1)]
    all_gather x2 -> x1, waiting for transfers between devices: 93.2 us -> 0.01 us  [body(): target = lax.all_gather(own, 'row', axis=0)]
    all_gather x2 -> x0, local copies, waits for them, and re-layouts: 61.3 us -> none  [the longest x1 40.3 us: body(): target_rows = lax.all_gather(entities, 'row', axis=1, tiled=True)]
    ppermute x0 -> x7, waiting for transfers between devices: none -> 48.9 us  [hop(): return lax.ppermute(array, BOTH, pairs)]
    dot_general x8 -> x0, matrix products: 39.3 us -> none  [the longest x1 9.68 us: bucket_terms(): jnp.einsum('kcn,knd->kcd', weights, negatives[1], preferred_element_type=...]
    unnamed x43 -> x12, local copies, waits for them, and re-layouts: 26.4 us -> 5.77 us
    ppermute x0 -> x7, starting transfers between devices: none -> 14.4 us  [hop(): return lax.ppermute(array, BOTH, pairs)]
  transfers between devices with their start and end apart: 2 -> 8, of which waited for: 2 -> 3; matrix products, arithmetic and copies ran while one was open for 18% -> 0% of each run, Pallas kernels for 0% -> 19%
where the time goes in v1:
time: 244 us; the launch traced here: 242 us
  Pallas kernels  117 us (48%)
  waiting for transfers between devices  49.6 us (20%)
  blocking collectives  40.4 us (17%)
  starting transfers between devices  14.4 us (6%)
  between operations  14.1 us (6%)
  local copies, waits for them, and re-layouts  5.86 us (2%)
    pallas_call x1, Pallas kernels, score_groups(): pl.pallas_call(group_kernel, out_shape=(jax.ShapeDtypeStruct((STEPS, 1, G...  71.2 us
    ppermute x7, waiting for transfers between devices, hop(): return lax.ppermute(array, BOTH, pairs)  48.9 us
    pallas_call x2, Pallas kernels, gather_rows(): pl.pallas_call(functools.partial(gather_kernel, count), out_shape=jax.Sha...  45.9 us
    all_to_all x1, blocking collectives, body(): parts = lax.all_to_all(grad.reshape(128, 8, WIDE), BOTH, 0, 0, tiled=True)  40.4 us
    ppermute x7, starting transfers between devices, hop(): return lax.ppermute(array, BOTH, pairs)  14.4 us
    unnamed x12, local copies, waits for them, and re-layouts  5.77 us
  transfers between devices with their start and end apart: 8, of which 3 were waited for; matrix products, arithmetic and copies ran while one was open for 0% of the time, Pallas kernels for 19%

profile of v1, /device:TPU:0, one launch (start us, length us, event | category | flops | bytes accessed | tf_op | source)
XLA Modules:
  0.0 242.4 jit_solution(1216919536429993795)
XLA Ops:
  7.2 0.0 all-gather.3.cloned.1.call-start
  7.2 0.7 all-gather.3.cloned.1.call-update
  7.9 4.0 %collective-permute-start = (bf16[2,200,1024]{2,1,0:T(8,128)(2,1)}, bf16[2,200,1024]{2,1,0:T(8,128)(2,1)S(1)}, u32[]{:S(2)}, u32[]{:S(2)}) collective-permute-start(bf16[2,200,1024]{2,1,0:T(8,128)(2,1)} %bitcast.19), channel_id=1, source_target_pairs={{0,1},{1,0},{2,3},{3,2},{4,5},{5,4},{6,7},{7,6},{8,9},{9,8},{10,11... | collective-permute-start | bytes 2457608 | tf_op jit(solution)/shard_map/ppermute | solution.py:29
  12.0 1.6 collective-permute-start.1
  13.5 25.8 %collective-permute-done.refs_1_ = bf16[2,200,1024]{2,1,0:T(8,128)(2,1)S(1)} collective-permute-done((bf16[2,200,1024]{2,1,0:T(8,128)(2,1)}, bf16[2,200,1024]{2,1,0:T(8,128)(2,1)S(1)}, u32[]{:S(2)}, u32[]{:S(2)}) %collective-permute-start) | collective-permute-done | bytes 819232 | tf_op jit(solution)/shard_map/ppermute | solution.py:29
  39.4 3.0 %collective-permute-start.4 = (bf16[2,200,1024]{2,1,0:T(8,128)(2,1)S(1)}, bf16[2,200,1024]{2,1,0:T(8,128)(2,1)S(1)}, u32[]{:S(2)}, u32[]{:S(2)}) collective-permute-start(bf16[2,200,1024]{2,1,0:T(8,128)(2,1)S(1)} %collective-permute-done.refs_1_), channel_id=1, source_target_pairs={{0,6},{1,7},{2,0},{3,1},{4,2},{5,3},{6,4},{7,5},{8,14},{9,15},{10,... | collective-permute-start | bytes 2457608 | tf_op jit(solution)/shard_map/ppermute | solution.py:29
  42.4 0.6 collective-permute-start.2
  43.1 1.4 collective-permute-start.3
  44.4 0.0 collective-permute-done.1.refs_2_
  44.4 0.0 collective-permute-start.5
  44.5 16.6 %collective-permute-done.4.refs_5_ = bf16[2,200,1024]{2,1,0:T(8,128)(2,1)S(1)} collective-permute-done((bf16[2,200,1024]{2,1,0:T(8,128)(2,1)S(1)}, bf16[2,200,1024]{2,1,0:T(8,128)(2,1)S(1)}, u32[]{:S(2)}, u32[]{:S(2)}) %collective-permute-start.4) | collective-permute-done | bytes 819232 | tf_op jit(solution)/shard_map/ppermute | solution.py:29
  61.1 3.7 %collective-permute-start.6 = (bf16[2,200,1024]{2,1,0:T(8,128)(2,1)S(1)}, bf16[2,200,1024]{2,1,0:T(8,128)(2,1)}, u32[]{:S(2)}, u32[]{:S(2)}) collective-permute-start(bf16[2,200,1024]{2,1,0:T(8,128)(2,1)S(1)} %collective-permute-done.4.refs_5_), channel_id=1, source_target_pairs={{0,6},{1,7},{2,0},{3,1},{4,2},{5,3},{6,4},{7,5},{8,14},{9,15},{10,... | collective-permute-start | bytes 2457608 | tf_op jit(solution)/shard_map/ppermute | solution.py:29
  64.8 1.2 copy-done.3
  66.0 0.7 copy-done.5
  66.7 16.7 %gather_rows.3.rel = bf16[4096,512]{1,0:T(8,128)(2,1)S(1)} custom-call(s32[4096]{0:T(1024)S(1)} %copy-done.5, s32[1]{0:T(128)} %constant.70.clone.1.order, bf16[2,200,1024]{2,1,0:T(8,128)(2,1)S(1)} %bitcast.23), custom_call_target="tpu_custom_call" | custom-call | bytes 28000000 | tf_op jit(solution)/shard_map/gather_rows/pallas_call | solution.py:90
  83.4 1.9 copy-done
  85.3 0.1 stack.44.order
  85.4 6.5 %collective-permute-done.6.refs_7_ = bf16[2,200,1024]{2,1,0:T(8,128)(2,1)} collective-permute-done((bf16[2,200,1024]{2,1,0:T(8,128)(2,1)S(1)}, bf16[2,200,1024]{2,1,0:T(8,128)(2,1)}, u32[]{:S(2)}, u32[]{:S(2)}) %collective-permute-start.6) | collective-permute-done | bytes 819232 | tf_op jit(solution)/shard_map/ppermute | solution.py:29
  91.9 29.3 %gather_rows.2.src = bf16[4096,512]{1,0:T(8,128)(2,1)S(1)} custom-call(s32[4096]{0:T(1024)S(1)} %copy-done.4, s32[8]{0:T(128)S(1)} %stack.44.order, bf16[2,200,1024]{2,1,0:T(8,128)(2,1)S(1)} %bitcast.22, bf16[2,200,1024]{2,1,0:T(8,128)(2,1)S(1)} %collective-permute-done.refs_1_, bf16[2,200,1024]{2,1,0:T(8,128)(2,1)S(1)} %collective-permute-done.1.refs_2_, ...), custom_call_target="tpu_custom_call" | custom-call | bytes 84000000 | tf_op jit(solution)/shard_map/gather_rows/pallas_call | solution.py:90
  121.1 2.0 copy-done.1
  123.1 71.2 %score_groups.1 = (f32[8,1,512]{2,1,0:T(1,128)}, f32[1024,512]{1,0:T(8,128)}) custom-call(s32[4096]{0:T(1024)} %index.5, s32[8]{0:T(128)} %blocks.1, bf16[16,2,200,1024]{3,2,1,0:T(8,128)(2,1)} %bitcast.26, bf16[4096,512]{1,0:T(8,128)(2,1)} %copy-done.1, bf16[4096,512]{1,0:T(8,128)(2,1)} %copy-done, s32[8,1,512]{2,1,0:T(1,128)} %bitcast.24), custom_call_target="tpu_custom_call" | custom-call | flops 20000000000 | bytes 24000000 | tf_op jit(solution)/shard_map/score_groups/pallas_call | solution.py:182
  194.3 40.4 %all_to_all.5 = f32[128,8,512]{2,1,0:T(8,128)S(1)} all-to-all(f32[128,8,512]{2,1,0:T(8,128)} %bitcast.25), channel_id=1, replica_groups=mesh['row'=16,'col'=8] {'row','col'}, dimensions={0} | all-to-all | bytes 4194304 | tf_op jit(solution)/shard_map/all_to_all | solution.py:220
  234.7 0.2 reduce_sum.9
  234.9 0.6 pad_maximum_fusion
  (13 shorter events, 0.0 us)
Async XLA Ops:
  7.2 84.7 %copy-start.2 = (bf16[2,1024,200]{1,2,0:T(8,128)(2,1)S(1)}, bf16[2,1024,200]{1,2,0:T(8,128)(2,1)}, u32[]{:S(2)}) copy-start(bf16[2,1024,200]{1,2,0:T(8,128)(2,1)} %param.6) | copy-start | bytes 2457604
  7.2 84.7 %copy-start.4 = (s32[4096]{0:T(1024)S(1)}, s32[4096]{0:T(1024)}, u32[]{:S(2)}) copy-start(s32[4096]{0:T(1024)} %index.3) | copy-start | bytes 49156
  7.2 115.9 %all-gather.3.cloned.1.call-start = ((), (), s32[]{:S(2)}) async-start(), calls=%async_computation.1 | async-start | bytes 13926400 | tf_op jit(solution)/shard_map/all_gather | solution.py:215
  7.9 31.4 %collective-permute-start = (bf16[2,200,1024]{2,1,0:T(8,128)(2,1)}, bf16[2,200,1024]{2,1,0:T(8,128)(2,1)S(1)}, u32[]{:S(2)}, u32[]{:S(2)}) collective-permute-start(bf16[2,200,1024]{2,1,0:T(8,128)(2,1)} %bitcast.19), channel_id=1, source_target_pairs={{0,1},{1,0},{2,3},{3,2},{4,5},{5,4},{6,7},{7,6},{8,9},{9,8},{10,11... | collective-permute-start | bytes 2457608 | tf_op jit(solution)/shard_map/ppermute | solution.py:29
  12.0 32.5 %collective-permute-start.1 = (bf16[2,200,1024]{2,1,0:T(8,128)(2,1)}, bf16[2,200,1024]{2,1,0:T(8,128)(2,1)S(1)}, u32[]{:S(2)}, u32[]{:S(2)}) collective-permute-start(bf16[2,200,1024]{2,1,0:T(8,128)(2,1)} %bitcast.20), channel_id=1, source_target_pairs={{0,2},{1,3},{2,4},{3,5},{4,6},{5,7},{6,0},{7,1},{8,10},{9,11},{10,... | collective-permute-start | bytes 2457608 | tf_op jit(solution)/shard_map/ppermute | solution.py:29
  39.4 21.7 %collective-permute-start.4 = (bf16[2,200,1024]{2,1,0:T(8,128)(2,1)S(1)}, bf16[2,200,1024]{2,1,0:T(8,128)(2,1)S(1)}, u32[]{:S(2)}, u32[]{:S(2)}) collective-permute-start(bf16[2,200,1024]{2,1,0:T(8,128)(2,1)S(1)} %collective-permute-done.refs_1_), channel_id=1, source_target_pairs={{0,6},{1,7},{2,0},{3,1},{4,2},{5,3},{6,4},{7,5},{8,14},{9,15},{10,... | collective-permute-start | bytes 2457608 | tf_op jit(solution)/shard_map/ppermute | solution.py:29
  42.4 43.0 %collective-permute-start.2 = (bf16[2,200,1024]{2,1,0:T(8,128)(2,1)}, bf16[2,200,1024]{2,1,0:T(8,128)(2,1)}, u32[]{:S(2)}, u32[]{:S(2)}) collective-permute-start(bf16[2,200,1024]{2,1,0:T(8,128)(2,1)} %bitcast.21), channel_id=1, source_target_pairs={{0,6},{1,7},{2,0},{3,1},{4,2},{5,3},{6,4},{7,5},{8,14},{9,15},{10,... | collective-permute-start | bytes 2457608 | tf_op jit(solution)/shard_map/ppermute | solution.py:29
  43.1 42.3 %collective-permute-start.3 = (bf16[2,200,1024]{2,1,0:T(8,128)(2,1)S(1)}, bf16[2,200,1024]{2,1,0:T(8,128)(2,1)}, u32[]{:S(2)}, u32[]{:S(2)}) collective-permute-start(bf16[2,200,1024]{2,1,0:T(8,128)(2,1)S(1)} %collective-permute-done.refs_1_), channel_id=1, source_target_pairs={{0,2},{1,3},{2,4},{3,5},{4,6},{5,7},{6,0},{7,1},{8,10},{9,11},{10,... | collective-permute-start | bytes 2457608 | tf_op jit(solution)/shard_map/ppermute | solution.py:29
  44.4 40.9 %collective-permute-start.5 = (bf16[2,200,1024]{2,1,0:T(8,128)(2,1)S(1)}, bf16[2,200,1024]{2,1,0:T(8,128)(2,1)}, u32[]{:S(2)}, u32[]{:S(2)}) collective-permute-start(bf16[2,200,1024]{2,1,0:T(8,128)(2,1)S(1)} %collective-permute-done.1.refs_2_), channel_id=1, source_target_pairs={{0,2},{1,3},{2,4},{3,5},{4,6},{5,7},{6,0},{7,1},{8,10},{9,11},{10,... | collective-permute-start | bytes 2457608 | tf_op jit(solution)/shard_map/ppermute | solution.py:29
  61.1 30.7 %collective-permute-start.6 = (bf16[2,200,1024]{2,1,0:T(8,128)(2,1)S(1)}, bf16[2,200,1024]{2,1,0:T(8,128)(2,1)}, u32[]{:S(2)}, u32[]{:S(2)}) collective-permute-start(bf16[2,200,1024]{2,1,0:T(8,128)(2,1)S(1)} %collective-permute-done.4.refs_5_), channel_id=1, source_target_pairs={{0,6},{1,7},{2,0},{3,1},{4,2},{5,3},{6,4},{7,5},{8,14},{9,15},{10,... | collective-permute-start | bytes 2457608 | tf_op jit(solution)/shard_map/ppermute | solution.py:29
  64.8 1.2 copy-start.3
  66.0 0.7 copy-start.5
  83.3 1.9 copy-start
  121.1 2.0 copy-start.1
Sparse Core Ops, SparseCore 0:
  9.7 84.6 all-gather.2

commit v2 on v1

v2 whole, which is shorter than its diff:
```python
import functools

import jax
import jax.numpy as jnp
from jax import lax
from jax.experimental import pallas as pl
from jax.experimental.pallas import tpu as pltpu
from jax.sharding import PartitionSpec as P

F32, BF16 = jnp.float32, jnp.bfloat16
SHARD = 1024
EDGES = 4096
GROUP = 512
NEGB = 512
HALF = 256
WIDE = 2 * HALF
DIM = 200
NREL = 1024
STEPS = EDGES // GROUP
BOTH = ("row", "col")


def hop(array, dy=0, flip=0):
    pairs = []
    for r in range(16):
        for c in range(8):
            y, h = c // 2, c % 2
            pairs.append((r * 8 + c, r * 8 + ((y + dy) % 4) * 2 + (h ^ flip)))
    return lax.ppermute(array, BOTH, pairs)


def column_shards(own):
    tie = lax.optimization_barrier

    def ring(held):
        near = tie((hop(held, dy=1), hop(held, dy=-1)))
        far = hop(near[0][:1], dy=1), hop(near[1][1:], dy=-1)
        return near, far

    pair = hop(own, flip=1)
    near, far = ring(own)
    pair, *far = tie((pair, *far))
    pair_near, pair_far = ring(pair)
    pieces = [(own, 0, None), (near[0], 1, None), (near[1], 2, None), (far[0], 3, 0), (far[1], 3, 1)]
    pieces += [(pair, 4, None), (pair_near[0], 5, None), (pair_near[1], 6, None), (pair_far[0], 7, 0), (pair_far[1], 7, 1)]
    c = lax.axis_index("col")
    y, h = c // 2, c % 2
    order = jnp.stack([((y + dy) % 4) * 2 + (h ^ flip) for flip in (0, 1) for dy in (0, -1, 1, 2)])
    return pieces, order.astype(jnp.int32)


def fill_rows(columns, start, table):
    def tile(t, carry):
        n = pl.multiple_of(t * 128, 128)
        for part in range(2):
            head = columns[part, 0:128, pl.ds(n, 128)].astype(F32)
            tail = columns[part, 128:DIM, pl.ds(n, 128)].astype(F32)
            tail = jnp.concatenate([tail, jnp.zeros((HALF - DIM, 128), F32)], 0)
            at = part * HALF
            table[pl.ds(start + n, 128), at : at + 128] = head.T
            table[pl.ds(start + n, 128), at + 128 : at + HALF] = tail.T
        return carry

    lax.fori_loop(0, SHARD // 128, tile, 0)


def pick_rows(index, first, table, rows, unroll=16):
    def step(i, carry):
        b = i * unroll
        values = [table[pl.ds(index[first + b + u], 1), :] for u in range(unroll)]
        for u in range(0, unroll, 8):
            rows[pl.ds(pl.multiple_of(b + u, 8), 8), :] = jnp.concatenate(values[u : u + 8], 0)
        return carry

    lax.fori_loop(0, GROUP // unroll, step, 0)


def gather_kernel(places, index, order, *refs):
    count = len(places)
    pieces, out = refs[:count], refs[count]
    held, table, rows, sem = refs[count + 1 :]
    g = pl.program_id(0)

    @pl.when(g == 0)
    def _():
        copies = []
        for piece, (slot, part) in zip(pieces, places):
            into = held.at[slot] if part is None else held.at[slot, pl.ds(part, 1)]
            copies.append(pltpu.make_async_copy(piece, into, sem.at[len(copies)]))
            copies[-1].start()
        for j, (slot, part) in enumerate(places):
            copies[j].wait()
            if part != 0:
                fill_rows(held.at[slot], pl.multiple_of(order[slot] * SHARD, SHARD), table)

    pick_rows(index, g * GROUP, table, rows)
    out[...] = rows[...].astype(BF16)


def gather_rows(pieces, order, index):
    places = tuple((slot, part) for _, slot, part in pieces)
    count = places[-1][0] + 1
    return pl.pallas_call(
        functools.partial(gather_kernel, places),
        out_shape=jax.ShapeDtypeStruct((EDGES, WIDE), BF16),
        grid_spec=pltpu.PrefetchScalarGridSpec(
            num_scalar_prefetch=2,
            grid=(STEPS,),
            in_specs=[pl.BlockSpec(memory_space=pl.ANY)] * len(places),
            out_specs=pl.BlockSpec((GROUP, WIDE), lambda g, *_: (g, 0)),
            scratch_shapes=[
                pltpu.VMEM((count, 2, DIM, SHARD), BF16),
                pltpu.VMEM((count * SHARD, WIDE), F32),
                pltpu.VMEM((GROUP, WIDE), F32),
                pltpu.SemaphoreType.DMA((len(places),)),
            ],
        ),
        compiler_params=pltpu.CompilerParams(vmem_limit_bytes=(8 + 4 * count) << 20),
        cost_estimate=pl.CostEstimate(flops=0, bytes_accessed=(5 + 2 * count) * 4_000_000, transcendentals=0),
        name="gather_rows",
    )(index, order, *[piece for piece, _, _ in pieces])


BLOCK = 256


def group_kernel(index, blocks, target, src, rel, rel_ids, loss, keep, give, held, table, rows, negs, terms, sem):
    g = pl.program_id(0)

    @pl.when(g == 0)
    def _():
        copies = [pltpu.make_async_copy(target.at[j], held.at[j], sem.at[j]) for j in range(16)]
        for copy in copies:
            copy.start()
        negs[...] = jnp.zeros_like(negs)
        keep[...] = jnp.zeros_like(keep)
        give[...] = jnp.zeros_like(give)
        for j in range(16):
            copies[j].wait()
            fill_rows(held.at[j], j * SHARD, table)

    @pl.when(g == 0)
    def _():
        pick_rows(index, 0, table, rows)
    block = blocks[g]
    half = pl.multiple_of((block % 2) * NEGB, NEGB)
    for part in range(2):
        negs[part * HALF : part * HALF + DIM, :] = held[block // 2, part, :, pl.ds(half, NEGB)]

    def piece(i, carry):
        at = pl.ds(pl.multiple_of(i * BLOCK, BLOCK), BLOCK)
        s = [src[at, k * 128 : (k + 1) * 128].astype(F32) for k in range(4)]
        w = [rel[at, k * 128 : (k + 1) * 128].astype(F32) for k in range(4)]
        o = [rows[at, k * 128 : (k + 1) * 128] for k in range(4)]
        q = [s[0] * w[0] - s[2] * w[2], s[1] * w[1] - s[3] * w[3], s[0] * w[2] + s[2] * w[0], s[1] * w[3] + s[3] * w[1]]
        pos = jnp.sum((q[0] * o[0] + q[1] * o[1]) + (q[2] * o[2] + q[3] * o[3]), axis=1, keepdims=True)
        qb = jnp.concatenate([v.astype(BF16) for v in q], axis=1)
        score = lax.dot_general(qb, negs[...], (((1,), (0,)), ((), ())), preferred_element_type=F32)
        low = jnp.exp(-jnp.abs(score))
        up = 1.0 + low
        weight = (jnp.where(score >= 0, 1.0 / NEGB, low * (1.0 / NEGB)) / up).astype(BF16)
        peak = jnp.maximum(score, 0.0)
        excess, total = low[:, 0:128], peak[:, 0:128]
        for k in range(1, 4):
            cut = slice(k * 128, (k + 1) * 128)
            excess = excess * up[:, cut] + low[:, cut]
            total = total + peak[:, cut]
        pull_low = jnp.exp(-jnp.abs(pos))
        pull = jnp.where(pos >= 0, pull_low, 1.0) / (1.0 + pull_low)
        pos_loss = jnp.maximum(-pos, 0.0) + jnp.log1p(pull_low)
        loss_part = (total + jnp.log1p(excess)) * (1.0 / NEGB) + pos_loss * (1.0 / 128)
        loss[0, :, at] = jnp.sum(loss_part.T, axis=0, keepdims=True)
        gneg = lax.dot_general(weight, negs[...], (((1,), (1,)), ((), ())), preferred_element_type=F32)
        d = [gneg[:, k * 128 : (k + 1) * 128] - pull * o[k] for k in range(4)]
        term = [d[0] * s[0] + d[2] * s[2], d[1] * s[1] + d[3] * s[3], d[2] * s[0] - d[0] * s[2], d[3] * s[1] - d[1] * s[3]]
        for k in range(4):
            terms[at, k * 128 : (k + 1) * 128] = term[k].astype(BF16)
        return carry

    nxt = jnp.minimum(g + 1, STEPS - 1) * GROUP
    for i in range(GROUP // BLOCK):
        piece(i, 0)
        for b in range(i * BLOCK, (i + 1) * BLOCK, 8):
            rows[b : b + 8, :] = jnp.concatenate([table[pl.ds(index[nxt + b + u], 1), :] for u in range(8)], 0)
    ids = rel_ids[0]

    hot = lax.broadcasted_iota(jnp.int32, (NREL, GROUP), 0) == ids
    hot = jnp.where(hot, 1.0, 0.0).astype(BF16)
    grad = jnp.dot(hot, terms[...], preferred_element_type=F32)
    keep[...] += grad[: NREL // 2]
    give[...] += grad[NREL // 2 :]


def score_groups(target, dst_index, neg_block, src, rel, places):
    return pl.pallas_call(
        group_kernel,
        out_shape=(
            jax.ShapeDtypeStruct((STEPS, 1, GROUP), F32),
            jax.ShapeDtypeStruct((NREL // 2, WIDE), F32),
            jax.ShapeDtypeStruct((NREL // 2, WIDE), F32),
        ),
        grid_spec=pltpu.PrefetchScalarGridSpec(
            num_scalar_prefetch=2,
            grid=(STEPS,),
            in_specs=[
                pl.BlockSpec(memory_space=pl.ANY),
                pl.BlockSpec((GROUP, WIDE), lambda g, *_: (g, 0)),
                pl.BlockSpec((GROUP, WIDE), lambda g, *_: (g, 0)),
                pl.BlockSpec((1, 1, GROUP), lambda g, *_: (g, 0, 0)),
            ],
            out_specs=[
                pl.BlockSpec((1, 1, GROUP), lambda g, *_: (g, 0, 0)),
                pl.BlockSpec((NREL // 2, WIDE), lambda g, *_: (0, 0)),
                pl.BlockSpec((NREL // 2, WIDE), lambda g, *_: (0, 0)),
            ],
            scratch_shapes=[
                pltpu.VMEM((16, 2, DIM, SHARD), BF16),
                pltpu.VMEM((16 * SHARD, WIDE), F32),
                pltpu.VMEM((GROUP, WIDE), F32),
                pltpu.VMEM((WIDE, NEGB), BF16),
                pltpu.VMEM((GROUP, WIDE), BF16),
                pltpu.SemaphoreType.DMA((16,)),
            ],
        ),
        compiler_params=pltpu.CompilerParams(vmem_limit_bytes=60 << 20),
        cost_estimate=pl.CostEstimate(flops=20_000_000_000, bytes_accessed=24_000_000, transcendentals=4_000_000),
        name="score_groups",
    )(dst_index, neg_block, target, src, rel, places.reshape(STEPS, 1, GROUP))


def sum_at_owner(keep, give):
    half = keep + lax.ppermute(give, BOTH, [(d, d ^ 8) for d in range(128)])
    groups = [[a * 16 + core * 8 + c for a in range(8) for c in range(8)] for core in range(2)]
    parts = lax.all_to_all(half.reshape(64, 8, WIDE), BOTH, 0, 0, axis_index_groups=groups, tiled=True)
    return jnp.sum(parts, axis=0)


def body(entities, relations, src_index, dst_index, rel_index, neg_block):
    own = jnp.swapaxes(entities, 1, 2)
    target = lax.all_gather(own, "row", axis=0)
    rel = gather_rows([(jnp.swapaxes(relations, 1, 2), 0, None)], jnp.zeros((1,), jnp.int32), rel_index)
    pieces, order = column_shards(own)
    src = gather_rows(pieces, order, src_index)
    core = lax.axis_index("row") % 2
    places = (((rel_index >> 6) & 1) ^ core) * 512 + (rel_index >> 7) * 64 + (rel_index & 63)
    loss, keep, give = score_groups(target, dst_index, neg_block, src, rel, places)
    share = sum_at_owner(keep, give)
    share = jnp.stack([share[:, :DIM], share[:, HALF : HALF + DIM]])
    return loss.reshape(EDGES), share


def solution(mesh):
    placed = (
        P(None, BOTH, None),
        P(),
        P(BOTH),
        P(BOTH),
        P(BOTH),
        P(BOTH),
    )
    return jax.shard_map(
        body,
        mesh=mesh,
        in_specs=placed,
        out_specs=(P(BOTH), P(None, BOTH, None)),
        check_vma=False,
    )
```

time: 244 us -> 193 us (0.79)
  Pallas kernels: 117 us -> 71.7 us
  blocking collectives: 40.4 us -> 28.2 us
  local copies, waits for them, and re-layouts: 5.86 us -> 13.7 us
    pallas_call x1, Pallas kernels: 71.2 us -> 41.3 us  [score_groups(): pl.pallas_call(group_kernel, out_shape=(jax.ShapeDtypeStruct((STEPS, 1, G...]
    pallas_call x2, Pallas kernels: 45.9 us -> 30.5 us  [gather_rows(): pl.pallas_call(functools.partial(gather_kernel, places), out_shape=jax.Sh...]
    all_to_all x1, blocking collectives: 40.4 us -> 28.2 us  [sum_at_owner(): lax.all_to_all(half.reshape(64, 8, WIDE), BOTH, 0, 0, axis_index_groups=g...]
    unnamed x12 -> x28, local copies, waits for them, and re-layouts: 5.77 us -> 11.9 us
    ppermute x7 -> x9, waiting for transfers between devices: 48.9 us -> 43.9 us  [hop(): return lax.ppermute(array, BOTH, pairs)]
    ppermute x0 -> x1, waiting for transfers between devices: none -> 2.86 us  [sum_at_owner(): half = keep + lax.ppermute(give, BOTH, [(d, d ^ 8) for d in range(128)])]
    ppermute x7 -> x9, starting transfers between devices: 14.4 us -> 14.4 us  [hop(): return lax.ppermute(array, BOTH, pairs)]
  transfers between devices with their start and end apart: 8 -> 11, of which waited for: 3 -> 6; matrix products, arithmetic and copies ran while one was open for 0% -> 1% of each run, Pallas kernels for 19% -> 16%
where the time goes in v2:
time: 193 us; the launch traced here: 192 us
  Pallas kernels  71.7 us (37%)
  waiting for transfers between devices  47.5 us (25%)
  blocking collectives  28.2 us (15%)
  starting transfers between devices  14.5 us (8%)
  between operations  14.2 us (7%)
  local copies, waits for them, and re-layouts  13.7 us (7%)
  other arithmetic  2.76 us (1%)
    ppermute x9, waiting for transfers between devices, hop(): return lax.ppermute(array, BOTH, pairs)  43.9 us
    pallas_call x1, Pallas kernels, score_groups(): pl.pallas_call(group_kernel, out_shape=(jax.ShapeDtypeStruct((STEPS, 1, G...  41.3 us
    pallas_call x2, Pallas kernels, gather_rows(): pl.pallas_call(functools.partial(gather_kernel, places), out_shape=jax.Sh...  30.5 us
    all_to_all x1, blocking collectives, sum_at_owner(): lax.all_to_all(half.reshape(64, 8, WIDE), BOTH, 0, 0, axis_index_groups=g...  28.2 us
    ppermute x9, starting transfers between devices, hop(): return lax.ppermute(array, BOTH, pairs)  14.4 us
    unnamed x28, local copies, waits for them, and re-layouts  11.9 us
  transfers between devices with their start and end apart: 11, of which 6 were waited for; matrix products, arithmetic and copies ran while one was open for 1% of the time, Pallas kernels for 16%

profile of v2, /device:TPU:0, one launch (start us, length us, event | category | flops | bytes accessed | tf_op | source)
XLA Modules:
  0.0 192.5 jit_solution(4343751589675279830)
XLA Ops:
  7.9 3.2 %collective-permute-start.1 = (bf16[2,200,1024]{2,1,0:T(8,128)(2,1)}, bf16[2,200,1024]{2,1,0:T(8,128)(2,1)S(1)}, u32[]{:S(2)}, u32[]{:S(2)}) collective-permute-start(bf16[2,200,1024]{2,1,0:T(8,128)(2,1)} %bitcast.20), channel_id=1, source_target_pairs={{0,6},{1,7},{2,0},{3,1},{4,2},{5,3},{6,4},{7,5},{8,14},{9,15},{10,... | collective-permute-start | bytes 2457608 | tf_op jit(solution)/shard_map/ppermute | solution.py:29
  11.1 3.9 %collective-permute-start.2 = (bf16[2,200,1024]{2,1,0:T(8,128)(2,1)}, bf16[2,200,1024]{2,1,0:T(8,128)(2,1)S(1)}, u32[]{:S(2)}, u32[]{:S(2)}) collective-permute-start(bf16[2,200,1024]{2,1,0:T(8,128)(2,1)} %bitcast.22), channel_id=1, source_target_pairs={{0,1},{1,0},{2,3},{3,2},{4,5},{5,4},{6,7},{7,6},{8,9},{9,8},{10,11... | collective-permute-start | bytes 2457608 | tf_op jit(solution)/shard_map/ppermute | solution.py:29
  15.0 13.9 %collective-permute-done.1.refs_2_ = bf16[2,200,1024]{2,1,0:T(8,128)(2,1)S(1)} collective-permute-done((bf16[2,200,1024]{2,1,0:T(8,128)(2,1)}, bf16[2,200,1024]{2,1,0:T(8,128)(2,1)S(1)}, u32[]{:S(2)}, u32[]{:S(2)}) %collective-permute-start.1) | collective-permute-done | bytes 819232 | tf_op jit(solution)/shard_map/ppermute | solution.py:29
  28.9 3.3 %collective-permute-done.refs_1_ = bf16[2,200,1024]{2,1,0:T(8,128)(2,1)S(1)} collective-permute-done((bf16[2,200,1024]{2,1,0:T(8,128)(2,1)}, bf16[2,200,1024]{2,1,0:T(8,128)(2,1)S(1)}, u32[]{:S(2)}, u32[]{:S(2)}) %collective-permute-start) | collective-permute-done | bytes 819232 | tf_op jit(solution)/shard_map/ppermute | solution.py:29
  32.6 1.7 collective-permute-start.3
  34.4 10.8 %collective-permute-done.2.refs_5_ = bf16[2,200,1024]{2,1,0:T(8,128)(2,1)S(1)} collective-permute-done((bf16[2,200,1024]{2,1,0:T(8,128)(2,1)}, bf16[2,200,1024]{2,1,0:T(8,128)(2,1)S(1)}, u32[]{:S(2)}, u32[]{:S(2)}) %collective-permute-start.2) | collective-permute-done | bytes 819232 | tf_op jit(solution)/shard_map/ppermute | solution.py:29
  46.7 3.2 %collective-permute-start.6 = (bf16[2,200,1024]{2,1,0:T(8,128)(2,1)S(1)}, bf16[2,200,1024]{2,1,0:T(8,128)(2,1)S(1)}, u32[]{:S(2)}, u32[]{:S(2)}) collective-permute-start(bf16[2,200,1024]{2,1,0:T(8,128)(2,1)S(1)} %collective-permute-done.2.refs_5_), channel_id=1, source_target_pairs={{0,6},{1,7},{2,0},{3,1},{4,2},{5,3},{6,4},{7,5},{8,14},{9,15},{10,... | collective-permute-start | bytes 2457608 | tf_op jit(solution)/shard_map/ppermute | solution.py:29
  50.0 12.6 %collective-permute-done.6.refs_7_ = bf16[2,200,1024]{2,1,0:T(8,128)(2,1)S(1)} collective-permute-done((bf16[2,200,1024]{2,1,0:T(8,128)(2,1)S(1)}, bf16[2,200,1024]{2,1,0:T(8,128)(2,1)S(1)}, u32[]{:S(2)}, u32[]{:S(2)}) %collective-permute-start.6) | collective-permute-done | bytes 819232 | tf_op jit(solution)/shard_map/ppermute | solution.py:29
  62.6 3.3 %collective-permute-done.5.refs_6_ = bf16[2,200,1024]{2,1,0:T(8,128)(2,1)S(1)} collective-permute-done((bf16[2,200,1024]{2,1,0:T(8,128)(2,1)S(1)}, bf16[2,200,1024]{2,1,0:T(8,128)(2,1)S(1)}, u32[]{:S(2)}, u32[]{:S(2)}) %collective-permute-start.5) | collective-permute-done | bytes 819232 | tf_op jit(solution)/shard_map/ppermute | solution.py:29
  66.6 0.9 copy-done.3
  68.6 1.7 collective-permute-start.7
  70.4 1.2 copy-done.5
  71.5 11.6 %gather_rows.3.rel = bf16[4096,512]{1,0:T(8,128)(2,1)S(1)} custom-call(s32[4096]{0:T(1024)S(1)} %copy-done.12, s32[1]{0:T(128)} %constant.75.clone.1.order, bf16[2,200,1024]{2,1,0:T(8,128)(2,1)S(1)} %bitcast.24), custom_call_target="tpu_custom_call" | custom-call | bytes 28000000 | tf_op jit(solution)/shard_map/gather_rows/pallas_call | solution.py:103
  83.1 1.9 copy-done
  85.7 1.1 copy-done.4
  86.9 1.2 copy-done.7
  88.1 1.0 copy-done.9
  89.1 1.0 copy-done.11
  90.2 18.9 %gather_rows.2.src = bf16[4096,512]{1,0:T(8,128)(2,1)S(1)} custom-call(s32[4096]{0:T(1024)S(1)} %copy-done.13, s32[8]{0:T(128)S(1)} %stack.44.order, bf16[2,200,1024]{2,1,0:T(8,128)(2,1)S(1)} %bitcast.23, bf16[2,200,1024]{2,1,0:T(8,128)(2,1)S(1)} %collective-permute-done.refs_1_, bf16[2,200,1024]{2,1,0:T(8,128)(2,1)S(1)} %collective-permute-done.1.refs_2_, ...), custom_call_target="tpu_custom_call" | custom-call | bytes 84000000 | tf_op jit(solution)/shard_map/gather_rows/pallas_call | solution.py:103
  109.1 2.0 %copy-done.1 = bf16[4096,512]{1,0:T(8,128)(2,1)} copy-done((bf16[4096,512]{1,0:T(8,128)(2,1)}, bf16[4096,512]{1,0:T(8,128)(2,1)S(1)}, u32[]{:S(2)}) %copy-start.1) | copy-done | bytes 4194328
  111.1 41.3 %score_groups.1 = (f32[8,1,512]{2,1,0:T(1,128)}, f32[512,512]{1,0:T(8,128)}, f32[512,512]{1,0:T(8,128)}) custom-call(s32[4096]{0:T(1024)} %index.5, s32[8]{0:T(128)} %blocks.1, bf16[16,2,200,1024]{3,2,1,0:T(8,128)(2,1)} %bitcast.26, bf16[4096,512]{1,0:T(8,128)(2,1)} %copy-done.1, bf16[4096,512]{1,0:T(8,128)(2,1)} %copy-done, s32[8,1,512]{2,1,0:T(1,128)} %bitcast.25), custom_call_target="tpu_custom_call" | custom-call | flops 20000000000 | bytes 24000000 | tf_op jit(solution)/shard_map/score_groups/pallas_call | solution.py:195
  152.4 2.9 %collective-permute-done.9 = f32[512,512]{1,0:T(8,128)S(1)} collective-permute-done((f32[512,512]{1,0:T(8,128)}, f32[512,512]{1,0:T(8,128)S(1)}, u32[]{:S(2)}, u32[]{:S(2)}) %collective-permute-start.9) | collective-permute-done | bytes 1048608 | tf_op jit(solution)/shard_map/ppermute | solution.py:232
  155.3 1.4 add_bitcast_fusion
  156.7 28.2 %all_to_all.5 = f32[64,8,512]{2,1,0:T(8,128)S(1)} all-to-all(f32[64,8,512]{2,1,0:T(8,128)S(1)} %add_bitcast_fusion), channel_id=1, replica_groups={{0,1,2,3,4,5,6,7,16,17,18,19,20,21,22,23,32,33,34,35,36,37,38,39,48,49,..., dimensions={0} | all-to-all | bytes 2097152 | tf_op jit(solution)/shard_map/all_to_all | solution.py:234
  (41 shorter events, 6.1 us)
Async XLA Ops:
  7.2 63.2 %copy-start.12 = (s32[4096]{0:T(1024)S(1)}, s32[4096]{0:T(1024)}, u32[]{:S(2)}) copy-start(s32[4096]{0:T(1024)} %index.4) | copy-start | bytes 49156
  7.2 103.9 %all-gather.3.cloned.1.call-start = ((), (), s32[]{:S(2)}) async-start(), calls=%async_computation.1 | async-start | bytes 13926400 | tf_op jit(solution)/shard_map/all_gather | solution.py:240
  7.9 77.8 %copy-start.2 = (bf16[2,1024,200]{1,2,0:T(8,128)(2,1)S(1)}, bf16[2,1024,200]{1,2,0:T(8,128)(2,1)}, u32[]{:S(2)}) copy-start(bf16[2,1024,200]{1,2,0:T(8,128)(2,1)} %param.6) | copy-start | bytes 2457604
  7.9 77.8 %copy-start.13 = (s32[4096]{0:T(1024)S(1)}, s32[4096]{0:T(1024)}, u32[]{:S(2)}) copy-start(s32[4096]{0:T(1024)} %index.3) | copy-start | bytes 49156
  7.9 21.0 %collective-permute-start.1 = (bf16[2,200,1024]{2,1,0:T(8,128)(2,1)}, bf16[2,200,1024]{2,1,0:T(8,128)(2,1)S(1)}, u32[]{:S(2)}, u32[]{:S(2)}) collective-permute-start(bf16[2,200,1024]{2,1,0:T(8,128)(2,1)} %bitcast.20), channel_id=1, source_target_pairs={{0,6},{1,7},{2,0},{3,1},{4,2},{5,3},{6,4},{7,5},{8,14},{9,15},{10,... | collective-permute-start | bytes 2457608 | tf_op jit(solution)/shard_map/ppermute | solution.py:29
  11.1 21.1 %collective-permute-start = (bf16[2,200,1024]{2,1,0:T(8,128)(2,1)}, bf16[2,200,1024]{2,1,0:T(8,128)(2,1)S(1)}, u32[]{:S(2)}, u32[]{:S(2)}) collective-permute-start(bf16[2,200,1024]{2,1,0:T(8,128)(2,1)} %bitcast.21), channel_id=1, source_target_pairs={{0,2},{1,3},{2,4},{3,5},{4,6},{5,7},{6,0},{7,1},{8,10},{9,11},{10,... | collective-permute-start | bytes 2457608 | tf_op jit(solution)/shard_map/ppermute | solution.py:29
  11.1 34.1 %collective-permute-start.2 = (bf16[2,200,1024]{2,1,0:T(8,128)(2,1)}, bf16[2,200,1024]{2,1,0:T(8,128)(2,1)S(1)}, u32[]{:S(2)}, u32[]{:S(2)}) collective-permute-start(bf16[2,200,1024]{2,1,0:T(8,128)(2,1)} %bitcast.22), channel_id=1, source_target_pairs={{0,1},{1,0},{2,3},{3,2},{4,5},{5,4},{6,7},{7,6},{8,9},{9,8},{10,11... | collective-permute-start | bytes 2457608 | tf_op jit(solution)/shard_map/ppermute | solution.py:29
  32.3 12.9 %collective-permute-start.4 = (bf16[1,200,1024]{2,1,0:T(8,128)(2,1)S(1)}, bf16[1,200,1024]{2,1,0:T(8,128)(2,1)S(1)}, u32[]{:S(2)}, u32[]{:S(2)}) collective-permute-start(bf16[1,200,1024]{2,1,0:T(8,128)(2,1)S(1)} %slice.19), channel_id=1, source_target_pairs={{0,6},{1,7},{2,0},{3,1},{4,2},{5,3},{6,4},{7,5},{8,14},{9,15},{10,... | collective-permute-start | bytes 1228808 | tf_op jit(solution)/shard_map/ppermute | solution.py:29
  32.6 13.3 %collective-permute-start.3 = (bf16[1,200,1024]{2,1,0:T(8,128)(2,1)S(1)}, bf16[1,200,1024]{2,1,0:T(8,128)(2,1)S(1)}, u32[]{:S(2)}, u32[]{:S(2)}) collective-permute-start(bf16[1,200,1024]{2,1,0:T(8,128)(2,1)S(1)} %slice.18), channel_id=1, source_target_pairs={{0,2},{1,3},{2,4},{3,5},{4,6},{5,7},{6,0},{7,1},{8,10},{9,11},{10,... | collective-permute-start | bytes 1228808 | tf_op jit(solution)/shard_map/ppermute | solution.py:29
  45.2 21.5 %copy-start.6 = (bf16[2,200,1024]{2,1,0:T(8,128)(2,1)}, bf16[2,200,1024]{2,1,0:T(8,128)(2,1)S(1)}, u32[]{:S(2)}) copy-start(bf16[2,200,1024]{2,1,0:T(8,128)(2,1)S(1)} %collective-permute-done.2.refs_5_) | copy-start | bytes 2457604
  45.2 0.8 copy-start.8
  46.7 15.9 %collective-permute-start.6 = (bf16[2,200,1024]{2,1,0:T(8,128)(2,1)S(1)}, bf16[2,200,1024]{2,1,0:T(8,128)(2,1)S(1)}, u32[]{:S(2)}, u32[]{:S(2)}) collective-permute-start(bf16[2,200,1024]{2,1,0:T(8,128)(2,1)S(1)} %collective-permute-done.2.refs_5_), channel_id=1, source_target_pairs={{0,6},{1,7},{2,0},{3,1},{4,2},{5,3},{6,4},{7,5},{8,14},{9,15},{10,... | collective-permute-start | bytes 2457608 | tf_op jit(solution)/shard_map/ppermute | solution.py:29
  49.9 15.9 %collective-permute-start.5 = (bf16[2,200,1024]{2,1,0:T(8,128)(2,1)S(1)}, bf16[2,200,1024]{2,1,0:T(8,128)(2,1)S(1)}, u32[]{:S(2)}, u32[]{:S(2)}) collective-permute-start(bf16[2,200,1024]{2,1,0:T(8,128)(2,1)S(1)} %collective-permute-done.2.refs_5_), channel_id=1, source_target_pairs={{0,2},{1,3},{2,4},{3,5},{4,6},{5,7},{6,0},{7,1},{8,10},{9,11},{10,... | collective-permute-start | bytes 2457608 | tf_op jit(solution)/shard_map/ppermute | solution.py:29
  66.6 0.9 copy-start.3
  68.3 17.4 %collective-permute-start.8 = (bf16[1,200,1024]{2,1,0:T(8,128)(2,1)}, bf16[1,200,1024]{2,1,0:T(8,128)(2,1)}, u32[]{:S(2)}, u32[]{:S(2)}) collective-permute-start(bf16[1,200,1024]{2,1,0:T(8,128)(2,1)} %slice.21), channel_id=1, source_target_pairs={{0,6},{1,7},{2,0},{3,1},{4,2},{5,3},{6,4},{7,5},{8,14},{9,15},{10,... | collective-permute-start | bytes 1228808 | tf_op jit(solution)/shard_map/ppermute | solution.py:29
  68.6 17.1 %collective-permute-start.7 = (bf16[1,200,1024]{2,1,0:T(8,128)(2,1)}, bf16[1,200,1024]{2,1,0:T(8,128)(2,1)}, u32[]{:S(2)}, u32[]{:S(2)}) collective-permute-start(bf16[1,200,1024]{2,1,0:T(8,128)(2,1)} %slice.20), channel_id=1, source_target_pairs={{0,2},{1,3},{2,4},{3,5},{4,6},{5,7},{6,0},{7,1},{8,10},{9,11},{10,... | collective-permute-start | bytes 1228808 | tf_op jit(solution)/shard_map/ppermute | solution.py:29
  70.4 1.2 copy-start.5
  83.1 1.9 %copy-start = (bf16[4096,512]{1,0:T(8,128)(2,1)}, bf16[4096,512]{1,0:T(8,128)(2,1)S(1)}, u32[]{:S(2)}) copy-start(bf16[4096,512]{1,0:T(8,128)(2,1)S(1)} %gather_rows.3.rel) | copy-start | bytes 12582916
  85.7 1.2 copy-start.4
  86.9 1.2 copy-start.7
  88.1 1.0 copy-start.9
  89.1 1.0 copy-start.11
  109.1 2.0 %copy-start.1 = (bf16[4096,512]{1,0:T(8,128)(2,1)}, bf16[4096,512]{1,0:T(8,128)(2,1)S(1)}, u32[]{:S(2)}) copy-start(bf16[4096,512]{1,0:T(8,128)(2,1)S(1)} %gather_rows.2.src) | copy-start | bytes 12582916
  152.3 3.0 %collective-permute-start.9 = (f32[512,512]{1,0:T(8,128)}, f32[512,512]{1,0:T(8,128)S(1)}, u32[]{:S(2)}, u32[]{:S(2)}) collective-permute-start(f32[512,512]{1,0:T(8,128)} %get-tuple-element.21), channel_id=1, source_target_pairs={{0,8},{1,9},{2,10},{3,11},{4,12},{5,13},{6,14},{7,15},{8,0},{9,1},... | collective-permute-start | bytes 3145736 | tf_op jit(solution)/shard_map/ppermute | solution.py:232
  (1 other events, 0.8 us)
Sparse Core Ops, SparseCore 0:
  9.7 87.4 all-gather.2

commit v3 on v2

--- a/solution.py
+++ b/solution.py
@@ -29,7 +29,7 @@
     return lax.ppermute(array, BOTH, pairs)
 
 
-def column_shards(own):
+def column_shards(own, first):
     tie = lax.optimization_barrier
 
     def ring(held):
@@ -39,14 +39,14 @@
 
     pair = hop(own, flip=1)
     near, far = ring(own)
-    pair, *far = tie((pair, *far))
+    pair, first, *far = tie((pair, first, *far))
     pair_near, pair_far = ring(pair)
     pieces = [(own, 0, None), (near[0], 1, None), (near[1], 2, None), (far[0], 3, 0), (far[1], 3, 1)]
     pieces += [(pair, 4, None), (pair_near[0], 5, None), (pair_near[1], 6, None), (pair_far[0], 7, 0), (pair_far[1], 7, 1)]
     c = lax.axis_index("col")
     y, h = c // 2, c % 2
     order = jnp.stack([((y + dy) % 4) * 2 + (h ^ flip) for flip in (0, 1) for dy in (0, -1, 1, 2)])
-    return pieces, order.astype(jnp.int32)
+    return pieces, order.astype(jnp.int32), first
 
 
 def fill_rows(columns, start, table):
@@ -115,7 +115,7 @@
                 pltpu.SemaphoreType.DMA((len(places),)),
             ],
         ),
-        compiler_params=pltpu.CompilerParams(vmem_limit_bytes=(8 + 4 * count) << 20),
+        compiler_params=pltpu.CompilerParams(vmem_limit_bytes=60 << 20),
         cost_estimate=pl.CostEstimate(flops=0, bytes_accessed=(5 + 2 * count) * 4_000_000, transcendentals=0),
         name="gather_rows",
     )(index, order, *[piece for piece, _, _ in pieces])
@@ -239,7 +239,7 @@
     own = jnp.swapaxes(entities, 1, 2)
     target = lax.all_gather(own, "row", axis=0)
     rel = gather_rows([(jnp.swapaxes(relations, 1, 2), 0, None)], jnp.zeros((1,), jnp.int32), rel_index)
-    pieces, order = column_shards(own)
+    pieces, order, rel = column_shards(own, rel)
     src = gather_rows(pieces, order, src_index)
     core = lax.axis_index("row") % 2
     places = (((rel_index >> 6) & 1) ^ core) * 512 + (rel_index >> 7) * 64 + (rel_index & 63)

time: 193 us -> 185 us (0.959)
  local copies, waits for them, and re-layouts: 13.7 us -> 3.92 us
  waiting for transfers between devices: 47.5 us -> 40.5 us
  Pallas kernels: 71.7 us -> 75.2 us
  starting transfers between devices: 14.5 us -> 17.2 us
  blocking collectives: 28.2 us -> 30.5 us
    unnamed x28 -> x14, local copies, waits for them, and re-layouts: 11.9 us -> 1.56 us
    ppermute x9, waiting for transfers between devices: 43.9 us -> 36.9 us  [hop(): return lax.ppermute(array, BOTH, pairs)]
    pallas_call x2, Pallas kernels: 30.5 us -> 33.9 us  [gather_rows(): pl.pallas_call(functools.partial(gather_kernel, places), out_shape=jax.Sh...]
    ppermute x9, starting transfers between devices: 14.4 us -> 17.1 us  [hop(): return lax.ppermute(array, BOTH, pairs)]
    all_to_all x1, blocking collectives: 28.2 us -> 30.5 us  [sum_at_owner(): lax.all_to_all(half.reshape(64, 8, WIDE), BOTH, 0, 0, axis_index_groups=g...]
  transfers between devices with their start and end apart: 11 -> 11, of which waited for: 6 -> 5; matrix products, arithmetic and copies ran while one was open for 1% -> 2% of each run, Pallas kernels for 16% -> 18%
where the time goes in v3:
time: 185 us; the launch traced here: 184 us
  Pallas kernels  75.2 us (41%)
  waiting for transfers between devices  40.5 us (22%)
  blocking collectives  30.5 us (16%)
  starting transfers between devices  17.2 us (9%)
  between operations  14.1 us (8%)
  local copies, waits for them, and re-layouts  3.92 us (2%)
  other arithmetic  2.75 us (1%)
    pallas_call x1, Pallas kernels, score_groups(): pl.pallas_call(group_kernel, out_shape=(jax.ShapeDtypeStruct((STEPS, 1, G...  41.3 us
    ppermute x9, waiting for transfers between devices, hop(): return lax.ppermute(array, BOTH, pairs)  36.9 us
    pallas_call x2, Pallas kernels, gather_rows(): pl.pallas_call(functools.partial(gather_kernel, places), out_shape=jax.Sh...  33.9 us
    all_to_all x1, blocking collectives, sum_at_owner(): lax.all_to_all(half.reshape(64, 8, WIDE), BOTH, 0, 0, axis_index_groups=g...  30.5 us
    ppermute x9, starting transfers between devices, hop(): return lax.ppermute(array, BOTH, pairs)  17.1 us
  transfers between devices with their start and end apart: 11, of which 5 were waited for; matrix products, arithmetic and copies ran while one was open for 2% of the time, Pallas kernels for 18%

profile of v3, /device:TPU:0, one launch (start us, length us, event | category | flops | bytes accessed | tf_op | source)
XLA Modules:
  0.0 184.3 jit_solution(11438683105972407247)
XLA Ops:
  7.2 0.7 all-gather.3.cloned.1.call-update
  7.9 1.7 collective-permute-start
  9.6 1.6 collective-permute-start.1
  11.2 4.0 %collective-permute-start.2 = (bf16[2,200,1024]{2,1,0:T(8,128)(2,1)}, bf16[2,200,1024]{2,1,0:T(8,128)(2,1)}, u32[]{:S(2)}, u32[]{:S(2)}) collective-permute-start(bf16[2,200,1024]{2,1,0:T(8,128)(2,1)} %bitcast.22), channel_id=1, source_target_pairs={{0,1},{1,0},{2,3},{3,2},{4,5},{5,4},{6,7},{7,6},{8,9},{9,8},{10,11... | collective-permute-start | bytes 2457608 | tf_op jit(solution)/shard_map/ppermute | solution.py:29
  15.2 14.4 %collective-permute-done.refs_1_ = bf16[2,200,1024]{2,1,0:T(8,128)(2,1)S(1)} collective-permute-done((bf16[2,200,1024]{2,1,0:T(8,128)(2,1)}, bf16[2,200,1024]{2,1,0:T(8,128)(2,1)S(1)}, u32[]{:S(2)}, u32[]{:S(2)}) %collective-permute-start) | collective-permute-done | bytes 819232 | tf_op jit(solution)/shard_map/ppermute | solution.py:29
  29.6 1.6 collective-permute-start.3
  31.3 1.7 collective-permute-start.4
  33.0 14.0 %gather_rows.2.rel = bf16[4096,512]{1,0:T(8,128)(2,1)} custom-call(s32[4096]{0:T(1024)} %index.3, s32[1]{0:T(128)} %constant.75.clone.1.order, bf16[2,200,1024]{2,1,0:T(8,128)(2,1)} %bitcast.24), custom_call_target="tpu_custom_call" | custom-call | bytes 28000000 | tf_op jit(solution)/shard_map/gather_rows/pallas_call | solution.py:103
  47.0 0.8 copy-done.4
  47.8 0.8 copy-done.5
  48.9 2.8 %collective-permute-start.6 = (bf16[2,200,1024]{2,1,0:T(8,128)(2,1)}, bf16[2,200,1024]{2,1,0:T(8,128)(2,1)S(1)}, u32[]{:S(2)}, u32[]{:S(2)}) collective-permute-start(bf16[2,200,1024]{2,1,0:T(8,128)(2,1)} %collective-permute-done.2.refs_5_), channel_id=1, source_target_pairs={{0,6},{1,7},{2,0},{3,1},{4,2},{5,3},{6,4},{7,5},{8,14},{9,15},{10,... | collective-permute-start | bytes 2457608 | tf_op jit(solution)/shard_map/ppermute | solution.py:29
  51.8 17.1 %collective-permute-done.5.refs_6_ = bf16[2,200,1024]{2,1,0:T(8,128)(2,1)S(1)} collective-permute-done((bf16[2,200,1024]{2,1,0:T(8,128)(2,1)}, bf16[2,200,1024]{2,1,0:T(8,128)(2,1)S(1)}, u32[]{:S(2)}, u32[]{:S(2)}) %collective-permute-start.5) | collective-permute-done | bytes 819232 | tf_op jit(solution)/shard_map/ppermute | solution.py:29
  68.8 0.9 slice.20
  69.7 0.8 slice.21
  70.5 3.2 %collective-permute-start.8 = (bf16[1,200,1024]{2,1,0:T(8,128)(2,1)}, bf16[1,200,1024]{2,1,0:T(8,128)(2,1)}, u32[]{:S(2)}, u32[]{:S(2)}) collective-permute-start(bf16[1,200,1024]{2,1,0:T(8,128)(2,1)} %slice.21), channel_id=1, source_target_pairs={{0,6},{1,7},{2,0},{3,1},{4,2},{5,3},{6,4},{7,5},{8,14},{9,15},{10,... | collective-permute-start | bytes 1228808 | tf_op jit(solution)/shard_map/ppermute | solution.py:29
  73.7 0.7 stack.44.order
  74.4 0.6 and_add_fusion
  75.0 5.4 %collective-permute-done.7.refs_8_ = bf16[1,200,1024]{2,1,0:T(8,128)(2,1)} collective-permute-done((bf16[1,200,1024]{2,1,0:T(8,128)(2,1)}, bf16[1,200,1024]{2,1,0:T(8,128)(2,1)}, u32[]{:S(2)}, u32[]{:S(2)}) %collective-permute-start.7) | collective-permute-done | bytes 409632 | tf_op jit(solution)/shard_map/ppermute | solution.py:29
  80.5 20.0 %gather_rows.3.src = bf16[4096,512]{1,0:T(8,128)(2,1)} custom-call(s32[4096]{0:T(1024)} %index.4, s32[8]{0:T(128)} %stack.44.order, bf16[2,200,1024]{2,1,0:T(8,128)(2,1)} %bitcast.23, bf16[2,200,1024]{2,1,0:T(8,128)(2,1)} %copy-done, bf16[2,200,1024]{2,1,0:T(8,128)(2,1)} %copy-done.1, bf16[1,200,1024]{2,1,0:T(8,128)(2,1)} %copy-done.4, ...), custom_call_target="tpu_custom_call" | custom-call | bytes 84000000 | tf_op jit(solution)/shard_map/gather_rows/pallas_call | solution.py:103
  100.5 41.3 %score_groups.1 = (f32[8,1,512]{2,1,0:T(1,128)}, f32[512,512]{1,0:T(8,128)}, f32[512,512]{1,0:T(8,128)}) custom-call(s32[4096]{0:T(1024)} %index.5, s32[8]{0:T(128)} %blocks.1, bf16[16,2,200,1024]{3,2,1,0:T(8,128)(2,1)} %bitcast.26, bf16[4096,512]{1,0:T(8,128)(2,1)} %gather_rows.3.src, bf16[4096,512]{1,0:T(8,128)(2,1)} %gather_rows.2.rel, s32[8,1,512]{2,1,0:T(1,128)} %bitcast.25), custom_call_target="tpu_custom_call" | custom-call | flops 20000000000 | bytes 24000000 | tf_op jit(solution)/shard_map/score_groups/pallas_call | solution.py:195
  141.9 2.9 %collective-permute-done.9 = f32[512,512]{1,0:T(8,128)S(1)} collective-permute-done((f32[512,512]{1,0:T(8,128)}, f32[512,512]{1,0:T(8,128)S(1)}, u32[]{:S(2)}, u32[]{:S(2)}) %collective-permute-start.9) | collective-permute-done | bytes 1048608 | tf_op jit(solution)/shard_map/ppermute | solution.py:232
  144.8 1.4 add_bitcast_fusion
  146.2 30.5 %all_to_all.5 = f32[64,8,512]{2,1,0:T(8,128)S(1)} all-to-all(f32[64,8,512]{2,1,0:T(8,128)S(1)} %add_bitcast_fusion), channel_id=1, replica_groups={{0,1,2,3,4,5,6,7,16,17,18,19,20,21,22,23,32,33,34,35,36,37,38,39,48,49,..., dimensions={0} | all-to-all | bytes 2097152 | tf_op jit(solution)/shard_map/all_to_all | solution.py:234
  176.8 0.6 pad_maximum_fusion
  (27 shorter events, 0.8 us)
Async XLA Ops:
  7.2 93.3 %all-gather.3.cloned.1.call-start = ((), (), s32[]{:S(2)}) async-start(), calls=%async_computation.1 | async-start | bytes 13926400 | tf_op jit(solution)/shard_map/all_gather | solution.py:240
  7.9 66.5 %copy-start.6 = (s32[4096]{0:T(1024)S(1)}, s32[4096]{0:T(1024)}, u32[]{:S(2)}) copy-start(s32[4096]{0:T(1024)} %index.3) | copy-start | bytes 49156
  7.9 21.6 %collective-permute-start = (bf16[2,200,1024]{2,1,0:T(8,128)(2,1)}, bf16[2,200,1024]{2,1,0:T(8,128)(2,1)S(1)}, u32[]{:S(2)}, u32[]{:S(2)}) collective-permute-start(bf16[2,200,1024]{2,1,0:T(8,128)(2,1)} %bitcast.20), channel_id=1, source_target_pairs={{0,2},{1,3},{2,4},{3,5},{4,6},{5,7},{6,0},{7,1},{8,10},{9,11},{10,... | collective-permute-start | bytes 2457608 | tf_op jit(solution)/shard_map/ppermute | solution.py:29
  9.6 19.9 %collective-permute-start.1 = (bf16[2,200,1024]{2,1,0:T(8,128)(2,1)}, bf16[2,200,1024]{2,1,0:T(8,128)(2,1)S(1)}, u32[]{:S(2)}, u32[]{:S(2)}) collective-permute-start(bf16[2,200,1024]{2,1,0:T(8,128)(2,1)} %bitcast.21), channel_id=1, source_target_pairs={{0,6},{1,7},{2,0},{3,1},{4,2},{5,3},{6,4},{7,5},{8,14},{9,15},{10,... | collective-permute-start | bytes 2457608 | tf_op jit(solution)/shard_map/ppermute | solution.py:29
  11.2 35.7 %collective-permute-start.2 = (bf16[2,200,1024]{2,1,0:T(8,128)(2,1)}, bf16[2,200,1024]{2,1,0:T(8,128)(2,1)}, u32[]{:S(2)}, u32[]{:S(2)}) collective-permute-start(bf16[2,200,1024]{2,1,0:T(8,128)(2,1)} %bitcast.22), channel_id=1, source_target_pairs={{0,1},{1,0},{2,3},{3,2},{4,5},{5,4},{6,7},{7,6},{8,9},{9,8},{10,11... | collective-permute-start | bytes 2457608 | tf_op jit(solution)/shard_map/ppermute | solution.py:29
  29.5 44.2 %copy-start = (bf16[2,200,1024]{2,1,0:T(8,128)(2,1)}, bf16[2,200,1024]{2,1,0:T(8,128)(2,1)S(1)}, u32[]{:S(2)}) copy-start(bf16[2,200,1024]{2,1,0:T(8,128)(2,1)S(1)} %collective-permute-done.refs_1_) | copy-start | bytes 2457604
  29.6 44.2 %copy-start.1 = (bf16[2,200,1024]{2,1,0:T(8,128)(2,1)}, bf16[2,200,1024]{2,1,0:T(8,128)(2,1)S(1)}, u32[]{:S(2)}) copy-start(bf16[2,200,1024]{2,1,0:T(8,128)(2,1)S(1)} %collective-permute-done.1.refs_2_) | copy-start | bytes 2457604
  29.6 17.4 %collective-permute-start.3 = (bf16[1,200,1024]{2,1,0:T(8,128)(2,1)S(1)}, bf16[1,200,1024]{2,1,0:T(8,128)(2,1)S(1)}, u32[]{:S(2)}, u32[]{:S(2)}) collective-permute-start(bf16[1,200,1024]{2,1,0:T(8,128)(2,1)S(1)} %slice.18), channel_id=1, source_target_pairs={{0,2},{1,3},{2,4},{3,5},{4,6},{5,7},{6,0},{7,1},{8,10},{9,11},{10,... | collective-permute-start | bytes 1228808 | tf_op jit(solution)/shard_map/ppermute | solution.py:29
  31.3 16.5 %collective-permute-start.4 = (bf16[1,200,1024]{2,1,0:T(8,128)(2,1)S(1)}, bf16[1,200,1024]{2,1,0:T(8,128)(2,1)S(1)}, u32[]{:S(2)}, u32[]{:S(2)}) collective-permute-start(bf16[1,200,1024]{2,1,0:T(8,128)(2,1)S(1)} %slice.19), channel_id=1, source_target_pairs={{0,6},{1,7},{2,0},{3,1},{4,2},{5,3},{6,4},{7,5},{8,14},{9,15},{10,... | collective-permute-start | bytes 1228808 | tf_op jit(solution)/shard_map/ppermute | solution.py:29
  47.0 0.8 copy-start.4
  47.8 0.8 copy-start.5
  48.5 20.3 %collective-permute-start.5 = (bf16[2,200,1024]{2,1,0:T(8,128)(2,1)}, bf16[2,200,1024]{2,1,0:T(8,128)(2,1)S(1)}, u32[]{:S(2)}, u32[]{:S(2)}) collective-permute-start(bf16[2,200,1024]{2,1,0:T(8,128)(2,1)} %collective-permute-done.2.refs_5_), channel_id=1, source_target_pairs={{0,2},{1,3},{2,4},{3,5},{4,6},{5,7},{6,0},{7,1},{8,10},{9,11},{10,... | collective-permute-start | bytes 2457608 | tf_op jit(solution)/shard_map/ppermute | solution.py:29
  48.9 19.9 %collective-permute-start.6 = (bf16[2,200,1024]{2,1,0:T(8,128)(2,1)}, bf16[2,200,1024]{2,1,0:T(8,128)(2,1)S(1)}, u32[]{:S(2)}, u32[]{:S(2)}) collective-permute-start(bf16[2,200,1024]{2,1,0:T(8,128)(2,1)} %collective-permute-done.2.refs_5_), channel_id=1, source_target_pairs={{0,6},{1,7},{2,0},{3,1},{4,2},{5,3},{6,4},{7,5},{8,14},{9,15},{10,... | collective-permute-start | bytes 2457608 | tf_op jit(solution)/shard_map/ppermute | solution.py:29
  68.8 11.6 %copy-start.2 = (bf16[2,200,1024]{2,1,0:T(8,128)(2,1)}, bf16[2,200,1024]{2,1,0:T(8,128)(2,1)S(1)}, u32[]{:S(2)}) copy-start(bf16[2,200,1024]{2,1,0:T(8,128)(2,1)S(1)} %collective-permute-done.5.refs_6_) | copy-start | bytes 2457604
  68.8 11.6 %copy-start.3 = (bf16[2,200,1024]{2,1,0:T(8,128)(2,1)}, bf16[2,200,1024]{2,1,0:T(8,128)(2,1)S(1)}, u32[]{:S(2)}) copy-start(bf16[2,200,1024]{2,1,0:T(8,128)(2,1)S(1)} %collective-permute-done.6.refs_7_) | copy-start | bytes 2457604
  69.7 10.7 %collective-permute-start.7 = (bf16[1,200,1024]{2,1,0:T(8,128)(2,1)}, bf16[1,200,1024]{2,1,0:T(8,128)(2,1)}, u32[]{:S(2)}, u32[]{:S(2)}) collective-permute-start(bf16[1,200,1024]{2,1,0:T(8,128)(2,1)} %slice.20), channel_id=1, source_target_pairs={{0,2},{1,3},{2,4},{3,5},{4,6},{5,7},{6,0},{7,1},{8,10},{9,11},{10,... | collective-permute-start | bytes 1228808 | tf_op jit(solution)/shard_map/ppermute | solution.py:29
  70.5 10.0 %collective-permute-start.8 = (bf16[1,200,1024]{2,1,0:T(8,128)(2,1)}, bf16[1,200,1024]{2,1,0:T(8,128)(2,1)}, u32[]{:S(2)}, u32[]{:S(2)}) collective-permute-start(bf16[1,200,1024]{2,1,0:T(8,128)(2,1)} %slice.21), channel_id=1, source_target_pairs={{0,6},{1,7},{2,0},{3,1},{4,2},{5,3},{6,4},{7,5},{8,14},{9,15},{10,... | collective-permute-start | bytes 1228808 | tf_op jit(solution)/shard_map/ppermute | solution.py:29
  141.8 3.0 %collective-permute-start.9 = (f32[512,512]{1,0:T(8,128)}, f32[512,512]{1,0:T(8,128)S(1)}, u32[]{:S(2)}, u32[]{:S(2)}) collective-permute-start(f32[512,512]{1,0:T(8,128)} %get-tuple-element.23), channel_id=1, source_target_pairs={{0,8},{1,9},{2,10},{3,11},{4,12},{5,13},{6,14},{7,15},{8,0},{9,1},... | collective-permute-start | bytes 3145736 | tf_op jit(solution)/shard_map/ppermute | solution.py:232
Sparse Core Ops, SparseCore 0:
  9.7 87.4 all-gather.2

commit v4 on v3

--- a/solution.py
+++ b/solution.py
@@ -32,14 +32,14 @@
 def column_shards(own, first):
     tie = lax.optimization_barrier
 
-    def ring(held):
-        near = tie((hop(held, dy=1), hop(held, dy=-1)))
+    def ring(held, *rest):
+        near = tie((hop(held, dy=1), hop(held, dy=-1), *rest))
         far = hop(near[0][:1], dy=1), hop(near[1][1:], dy=-1)
         return near, far
 
     pair = hop(own, flip=1)
-    near, far = ring(own)
-    pair, first, *far = tie((pair, first, *far))
+    (*near, first), far = ring(own, first)
+    pair, *far = tie((pair, *far))
     pair_near, pair_far = ring(pair)
     pieces = [(own, 0, None), (near[0], 1, None), (near[1], 2, None), (far[0], 3, 0), (far[1], 3, 1)]
     pieces += [(pair, 4, None), (pair_near[0], 5, None), (pair_near[1], 6, None), (pair_far[0], 7, 0), (pair_far[1], 7, 1)]
@@ -53,15 +53,15 @@
     def tile(t, carry):
         n = pl.multiple_of(t * 128, 128)
         for part in range(2):
-            head = columns[part, 0:128, pl.ds(n, 128)].astype(F32)
+            head = columns[part, 0:128, pl.ds(n, 128)]
             tail = columns[part, 128:DIM, pl.ds(n, 128)].astype(F32)
-            tail = jnp.concatenate([tail, jnp.zeros((HALF - DIM, 128), F32)], 0)
+            tail = jnp.concatenate([tail, jnp.zeros((HALF - DIM, 128), F32)], 0).astype(BF16)
             at = part * HALF
-            table[pl.ds(start + n, 128), at : at + 128] = head.T
-            table[pl.ds(start + n, 128), at + 128 : at + HALF] = tail.T
+            table[pl.ds(start + n, 128), at : at + 128] = head.T.astype(F32)
+            table[pl.ds(start + n, 128), at + 128 : at + HALF] = tail.T.astype(F32)
         return carry
 
-    lax.fori_loop(0, SHARD // 128, tile, 0)
+    lax.fori_loop(0, SHARD // 128, tile, 0, unroll=8)
 
 
 def pick_rows(index, first, table, rows, unroll=16):
@@ -121,22 +121,26 @@
     )(index, order, *[piece for piece, _, _ in pieces])
 
 
+AHEAD = 3
 BLOCK = 256
-
-
-def group_kernel(index, blocks, target, src, rel, rel_ids, loss, keep, give, held, table, rows, negs, terms, sem):
+CHUNK = 16
+
+
+def group_kernel(index, blocks, target, src, rel, rel_ids, loss, keep, give, held, table, rows, negs, terms, query, wide, pull, losses, sem):
     g = pl.program_id(0)
 
     @pl.when(g == 0)
     def _():
         copies = [pltpu.make_async_copy(target.at[j], held.at[j], sem.at[j]) for j in range(16)]
-        for copy in copies:
+        for copy in copies[:AHEAD]:
             copy.start()
         negs[...] = jnp.zeros_like(negs)
         keep[...] = jnp.zeros_like(keep)
         give[...] = jnp.zeros_like(give)
         for j in range(16):
             copies[j].wait()
+            if j + AHEAD < 16:
+                copies[j + AHEAD].start()
             fill_rows(held.at[j], j * SHARD, table)
 
     @pl.when(g == 0)
@@ -147,41 +151,57 @@
     for part in range(2):
         negs[part * HALF : part * HALF + DIM, :] = held[block // 2, part, :, pl.ds(half, NEGB)]
 
-    def piece(i, carry):
-        at = pl.ds(pl.multiple_of(i * BLOCK, BLOCK), BLOCK)
-        s = [src[at, k * 128 : (k + 1) * 128].astype(F32) for k in range(4)]
-        w = [rel[at, k * 128 : (k + 1) * 128].astype(F32) for k in range(4)]
-        o = [rows[at, k * 128 : (k + 1) * 128] for k in range(4)]
+    nxt = jnp.minimum(g + 1, STEPS - 1) * GROUP
+    tiles = [slice(k * 128, (k + 1) * 128) for k in range(4)]
+
+    def queries(at):
+        s = [src[at, t].astype(F32) for t in tiles]
+        w = [rel[at, t].astype(F32) for t in tiles]
+        o = [rows[at, t] for t in tiles]
         q = [s[0] * w[0] - s[2] * w[2], s[1] * w[1] - s[3] * w[3], s[0] * w[2] + s[2] * w[0], s[1] * w[3] + s[3] * w[1]]
         pos = jnp.sum((q[0] * o[0] + q[1] * o[1]) + (q[2] * o[2] + q[3] * o[3]), axis=1, keepdims=True)
-        qb = jnp.concatenate([v.astype(BF16) for v in q], axis=1)
-        score = lax.dot_general(qb, negs[...], (((1,), (0,)), ((), ())), preferred_element_type=F32)
-        low = jnp.exp(-jnp.abs(score))
-        up = 1.0 + low
-        weight = (jnp.where(score >= 0, 1.0 / NEGB, low * (1.0 / NEGB)) / up).astype(BF16)
-        peak = jnp.maximum(score, 0.0)
-        excess, total = low[:, 0:128], peak[:, 0:128]
-        for k in range(1, 4):
-            cut = slice(k * 128, (k + 1) * 128)
-            excess = excess * up[:, cut] + low[:, cut]
-            total = total + peak[:, cut]
-        pull_low = jnp.exp(-jnp.abs(pos))
-        pull = jnp.where(pos >= 0, pull_low, 1.0) / (1.0 + pull_low)
-        pos_loss = jnp.maximum(-pos, 0.0) + jnp.log1p(pull_low)
-        loss_part = (total + jnp.log1p(excess)) * (1.0 / NEGB) + pos_loss * (1.0 / 128)
-        loss[0, :, at] = jnp.sum(loss_part.T, axis=0, keepdims=True)
-        gneg = lax.dot_general(weight, negs[...], (((1,), (1,)), ((), ())), preferred_element_type=F32)
-        d = [gneg[:, k * 128 : (k + 1) * 128] - pull * o[k] for k in range(4)]
+        for t, v in zip(tiles, q):
+            query[at, t] = v.astype(BF16)
+        low = jnp.exp(-jnp.abs(pos))
+        pull[at, :] = jnp.broadcast_to(jnp.where(pos >= 0, low, 1.0) / (1.0 + low), (CHUNK, 128))
+        losses[at, :] = jnp.broadcast_to((jnp.maximum(-pos, 0.0) + jnp.log1p(low)) * (1.0 / 128), (CHUNK, 128))
+
+    def weights(at):
+        for k, t in enumerate(tiles):
+            score = wide[at, t]
+            low = jnp.exp(-jnp.abs(score))
+            up = 1.0 + low
+            query[at, t] = (jnp.where(score >= 0, 1.0 / NEGB, low * (1.0 / NEGB)) / up).astype(BF16)
+            peak = jnp.maximum(score, 0.0)
+            excess = excess * up + low if k else low
+            total = total + peak if k else peak
+        losses[at, :] += (total + jnp.log1p(excess)) * (1.0 / NEGB)
+
+    def gradients(at):
+        s = [src[at, t].astype(F32) for t in tiles]
+        p = pull[at, :]
+        d = [wide[at, t] - p * rows[at, t] for t in tiles]
         term = [d[0] * s[0] + d[2] * s[2], d[1] * s[1] + d[3] * s[3], d[2] * s[0] - d[0] * s[2], d[3] * s[1] - d[1] * s[3]]
-        for k in range(4):
-            terms[at, k * 128 : (k + 1) * 128] = term[k].astype(BF16)
-        return carry
-
-    nxt = jnp.minimum(g + 1, STEPS - 1) * GROUP
-    for i in range(GROUP // BLOCK):
-        piece(i, 0)
-        for b in range(i * BLOCK, (i + 1) * BLOCK, 8):
+        for t, v in zip(tiles, term):
+            terms[at, t] = v.astype(BF16)
+        for b in range(at.start, at.stop, 8):
             rows[b : b + 8, :] = jnp.concatenate([table[pl.ds(index[nxt + b + u], 1), :] for u in range(8)], 0)
+
+    blocks_of = [slice(b, b + BLOCK) for b in range(0, GROUP, BLOCK)]
+    chunks_of = lambda block: [slice(c, c + CHUNK) for c in range(block.start, block.stop, CHUNK)]
+    for block in blocks_of:
+        for at in chunks_of(block):
+            queries(at)
+        wide[block, :] = jnp.dot(query[block, :], negs[...], preferred_element_type=F32)
+    for block in blocks_of:
+        for at in chunks_of(block):
+            weights(at)
+        wide[block, :] = lax.dot_general(query[block, :], negs[...], (((1,), (1,)), ((), ())), preferred_element_type=F32)
+    for block in blocks_of:
+        for at in chunks_of(block):
+            gradients(at)
+    for b in range(0, GROUP, 128):
+        loss[0, :, b : b + 128] = jnp.sum(losses[b : b + 128, :].T, axis=0, keepdims=True)
     ids = rel_ids[0]
 
     hot = lax.broadcasted_iota(jnp.int32, (NREL, GROUP), 0) == ids
@@ -219,6 +239,10 @@
                 pltpu.VMEM((GROUP, WIDE), F32),
                 pltpu.VMEM((WIDE, NEGB), BF16),
                 pltpu.VMEM((GROUP, WIDE), BF16),
+                pltpu.VMEM((GROUP, WIDE), BF16),
+                pltpu.VMEM((GROUP, WIDE), F32),
+                pltpu.VMEM((GROUP, 128), F32),
+                pltpu.VMEM((GROUP, 128), F32),
                 pltpu.SemaphoreType.DMA((16,)),
             ],
         ),

time: 185 us -> 169 us (0.914)
  Pallas kernels: 75.2 us -> 63.5 us
  blocking collectives: 30.5 us -> 25.8 us
  waiting for transfers between devices: 40.5 us -> 42.7 us
    pallas_call x1, Pallas kernels: 41.3 us -> 33.8 us  [score_groups(): pl.pallas_call(group_kernel, out_shape=(jax.ShapeDtypeStruct((STEPS, 1, G...]
    all_gather x1, waiting for transfers between devices: 0.02 us -> 7.36 us  [body(): target = lax.all_gather(own, 'row', axis=0)]
    ppermute x9, waiting for transfers between devices: 36.9 us -> 32 us  [hop(): return lax.ppermute(array, BOTH, pairs)]
    all_to_all x1, blocking collectives: 30.5 us -> 25.8 us  [sum_at_owner(): lax.all_to_all(half.reshape(64, 8, WIDE), BOTH, 0, 0, axis_index_groups=g...]
    pallas_call x2, Pallas kernels: 33.9 us -> 29.7 us  [gather_rows(): pl.pallas_call(functools.partial(gather_kernel, places), out_shape=jax.Sh...]
  transfers between devices with their start and end apart: 11 -> 11, of which waited for: 5 -> 7; matrix products, arithmetic and copies ran while one was open for 2% -> 2% of each run, Pallas kernels for 18% -> 18%
where the time goes in v4:
time: 169 us
  Pallas kernels  63.5 us (38%)
  waiting for transfers between devices  42.7 us (25%)
  blocking collectives  25.8 us (15%)
  starting transfers between devices  17.5 us (10%)
  between operations  14.1 us (8%)
  other arithmetic  2.75 us (2%)
  local copies, waits for them, and re-layouts  2.39 us (1%)
    pallas_call x1, Pallas kernels, score_groups(): pl.pallas_call(group_kernel, out_shape=(jax.ShapeDtypeStruct((STEPS, 1, G...  33.8 us
    ppermute x9, waiting for transfers between devices, hop(): return lax.ppermute(array, BOTH, pairs)  32 us
    pallas_call x2, Pallas kernels, gather_rows(): pl.pallas_call(functools.partial(gather_kernel, places), out_shape=jax.Sh...  29.7 us
    all_to_all x1, blocking collectives, sum_at_owner(): lax.all_to_all(half.reshape(64, 8, WIDE), BOTH, 0, 0, axis_index_groups=g...  25.8 us
    ppermute x9, starting transfers between devices, hop(): return lax.ppermute(array, BOTH, pairs)  17.2 us
    all_gather x1, waiting for transfers between devices, body(): target = lax.all_gather(own, 'row', axis=0)  7.36 us
  transfers between devices with their start and end apart: 11, of which 7 were waited for; matrix products, arithmetic and copies ran while one was open for 2% of the time, Pallas kernels for 18%

profile of v4, /device:TPU:0, one launch (start us, length us, event | category | flops | bytes accessed | tf_op | source)
XLA Modules:
  0.0 168.8 jit_solution(11695460172653462551)
XLA Ops:
  7.2 0.7 all-gather.3.cloned.1.call-update
  7.9 1.7 %collective-permute-start = (bf16[2,200,1024]{2,1,0:T(8,128)(2,1)}, bf16[2,200,1024]{2,1,0:T(8,128)(2,1)S(1)}, u32[]{:S(2)}, u32[]{:S(2)}) collective-permute-start(bf16[2,200,1024]{2,1,0:T(8,128)(2,1)} %bitcast.20), channel_id=1, source_target_pairs={{0,2},{1,3},{2,4},{3,5},{4,6},{5,7},{6,0},{7,1},{8,10},{9,11},{10,... | collective-permute-start | bytes 2457608 | tf_op jit(solution)/shard_map/ppermute | solution.py:29
  9.6 1.6 collective-permute-start.1
  11.2 4.0 %collective-permute-start.2 = (bf16[2,200,1024]{2,1,0:T(8,128)(2,1)}, bf16[2,200,1024]{2,1,0:T(8,128)(2,1)}, u32[]{:S(2)}, u32[]{:S(2)}) collective-permute-start(bf16[2,200,1024]{2,1,0:T(8,128)(2,1)} %bitcast.22), channel_id=1, source_target_pairs={{0,1},{1,0},{2,3},{3,2},{4,5},{5,4},{6,7},{7,6},{8,9},{9,8},{10,11... | collective-permute-start | bytes 2457608 | tf_op jit(solution)/shard_map/ppermute | solution.py:29
  15.2 13.6 %gather_rows.2.rel = bf16[4096,512]{1,0:T(8,128)(2,1)} custom-call(s32[4096]{0:T(1024)} %index.3, s32[1]{0:T(128)} %constant.75.clone.1.order, bf16[2,200,1024]{2,1,0:T(8,128)(2,1)} %bitcast.24), custom_call_target="tpu_custom_call" | custom-call | bytes 28000000 | tf_op jit(solution)/shard_map/gather_rows/pallas_call | solution.py:103
  28.8 0.7 collective-permute-done.refs_1_
  29.6 1.6 collective-permute-start.3
  31.3 1.7 %collective-permute-start.4 = (bf16[1,200,1024]{2,1,0:T(8,128)(2,1)S(1)}, bf16[1,200,1024]{2,1,0:T(8,128)(2,1)S(1)}, u32[]{:S(2)}, u32[]{:S(2)}) collective-permute-start(bf16[1,200,1024]{2,1,0:T(8,128)(2,1)S(1)} %slice.19), channel_id=1, source_target_pairs={{0,6},{1,7},{2,0},{3,1},{4,2},{5,3},{6,4},{7,5},{8,14},{9,15},{10,... | collective-permute-start | bytes 1228808 | tf_op jit(solution)/shard_map/ppermute | solution.py:29
  33.0 12.4 %collective-permute-done.2.refs_5_ = bf16[2,200,1024]{2,1,0:T(8,128)(2,1)} collective-permute-done((bf16[2,200,1024]{2,1,0:T(8,128)(2,1)}, bf16[2,200,1024]{2,1,0:T(8,128)(2,1)}, u32[]{:S(2)}, u32[]{:S(2)}) %collective-permute-start.2) | collective-permute-done | bytes 819232 | tf_op jit(solution)/shard_map/ppermute | solution.py:29
  45.5 3.2 %collective-permute-start.6 = (bf16[2,200,1024]{2,1,0:T(8,128)(2,1)}, bf16[2,200,1024]{2,1,0:T(8,128)(2,1)S(1)}, u32[]{:S(2)}, u32[]{:S(2)}) collective-permute-start(bf16[2,200,1024]{2,1,0:T(8,128)(2,1)} %collective-permute-done.2.refs_5_), channel_id=1, source_target_pairs={{0,6},{1,7},{2,0},{3,1},{4,2},{5,3},{6,4},{7,5},{8,14},{9,15},{10,... | collective-permute-start | bytes 2457608 | tf_op jit(solution)/shard_map/ppermute | solution.py:29
  48.8 14.3 %collective-permute-done.5.refs_6_ = bf16[2,200,1024]{2,1,0:T(8,128)(2,1)S(1)} collective-permute-done((bf16[2,200,1024]{2,1,0:T(8,128)(2,1)}, bf16[2,200,1024]{2,1,0:T(8,128)(2,1)S(1)}, u32[]{:S(2)}, u32[]{:S(2)}) %collective-permute-start.5) | collective-permute-done | bytes 819232 | tf_op jit(solution)/shard_map/ppermute | solution.py:29
  63.1 0.9 slice.20
  63.9 0.8 slice.21
  64.7 3.2 %collective-permute-start.8 = (bf16[1,200,1024]{2,1,0:T(8,128)(2,1)}, bf16[1,200,1024]{2,1,0:T(8,128)(2,1)}, u32[]{:S(2)}, u32[]{:S(2)}) collective-permute-start(bf16[1,200,1024]{2,1,0:T(8,128)(2,1)} %slice.21), channel_id=1, source_target_pairs={{0,6},{1,7},{2,0},{3,1},{4,2},{5,3},{6,4},{7,5},{8,14},{9,15},{10,... | collective-permute-start | bytes 1228808 | tf_op jit(solution)/shard_map/ppermute | solution.py:29
  68.0 0.7 stack.44.order
  68.6 0.6 and_add_fusion
  69.2 4.2 %collective-permute-done.7.refs_8_ = bf16[1,200,1024]{2,1,0:T(8,128)(2,1)} collective-permute-done((bf16[1,200,1024]{2,1,0:T(8,128)(2,1)}, bf16[1,200,1024]{2,1,0:T(8,128)(2,1)}, u32[]{:S(2)}, u32[]{:S(2)}) %collective-permute-start.7) | collective-permute-done | bytes 409632 | tf_op jit(solution)/shard_map/ppermute | solution.py:29
  73.8 16.1 %gather_rows.3.src = bf16[4096,512]{1,0:T(8,128)(2,1)} custom-call(s32[4096]{0:T(1024)} %index.4, s32[8]{0:T(128)} %stack.44.order, bf16[2,200,1024]{2,1,0:T(8,128)(2,1)} %bitcast.23, bf16[2,200,1024]{2,1,0:T(8,128)(2,1)} %copy-done, bf16[2,200,1024]{2,1,0:T(8,128)(2,1)} %copy-done.1, bf16[1,200,1024]{2,1,0:T(8,128)(2,1)} %copy-done.4, ...), custom_call_target="tpu_custom_call" | custom-call | bytes 84000000 | tf_op jit(solution)/shard_map/gather_rows/pallas_call | solution.py:103
  89.8 7.4 %all-gather.3.cloned.1.call-done = bf16[32,200,1024]{2,1,0:T(8,128)(2,1)} async-done(((bf16[2,200,1024]{2,1,0:T(8,128)(2,1)}), bf16[32,200,1024]{2,1,0:T(8,128)(2,1)}) %all-gather.3.cloned.1.call-update) | async-done | bytes 13107216 | tf_op jit(solution)/shard_map/all_gather | solution.py:264
  97.2 33.8 %score_groups.1 = (f32[8,1,512]{2,1,0:T(1,128)}, f32[512,512]{1,0:T(8,128)}, f32[512,512]{1,0:T(8,128)}) custom-call(s32[4096]{0:T(1024)} %index.5, s32[8]{0:T(128)} %blocks.1, bf16[16,2,200,1024]{3,2,1,0:T(8,128)(2,1)} %bitcast.26, bf16[4096,512]{1,0:T(8,128)(2,1)} %gather_rows.3.src, bf16[4096,512]{1,0:T(8,128)(2,1)} %gather_rows.2.rel, s32[8,1,512]{2,1,0:T(1,128)} %bitcast.25), custom_call_target="tpu_custom_call" | custom-call | flops 20000000000 | bytes 24000000 | tf_op jit(solution)/shard_map/score_groups/pallas_call | solution.py:215
  131.4 2.6 %collective-permute-done.9 = f32[512,512]{1,0:T(8,128)S(1)} collective-permute-done((f32[512,512]{1,0:T(8,128)}, f32[512,512]{1,0:T(8,128)S(1)}, u32[]{:S(2)}, u32[]{:S(2)}) %collective-permute-start.9) | collective-permute-done | bytes 1048608 | tf_op jit(solution)/shard_map/ppermute | solution.py:256
  134.0 1.4 add_bitcast_fusion
  135.4 25.8 %all_to_all.5 = f32[64,8,512]{2,1,0:T(8,128)S(1)} all-to-all(f32[64,8,512]{2,1,0:T(8,128)S(1)} %add_bitcast_fusion), channel_id=1, replica_groups={{0,1,2,3,4,5,6,7,16,17,18,19,20,21,22,23,32,33,34,35,36,37,38,39,48,49,..., dimensions={0} | all-to-all | bytes 2097152 | tf_op jit(solution)/shard_map/all_to_all | solution.py:258
  161.3 0.6 pad_maximum_fusion
  (27 shorter events, 1.0 us)
Async XLA Ops:
  7.2 90.0 %all-gather.3.cloned.1.call-start = ((), (), s32[]{:S(2)}) async-start(), calls=%async_computation.1 | async-start | bytes 13926400 | tf_op jit(solution)/shard_map/all_gather | solution.py:264
  7.9 21.6 %collective-permute-start = (bf16[2,200,1024]{2,1,0:T(8,128)(2,1)}, bf16[2,200,1024]{2,1,0:T(8,128)(2,1)S(1)}, u32[]{:S(2)}, u32[]{:S(2)}) collective-permute-start(bf16[2,200,1024]{2,1,0:T(8,128)(2,1)} %bitcast.20), channel_id=1, source_target_pairs={{0,2},{1,3},{2,4},{3,5},{4,6},{5,7},{6,0},{7,1},{8,10},{9,11},{10,... | collective-permute-start | bytes 2457608 | tf_op jit(solution)/shard_map/ppermute | solution.py:29
  9.6 19.9 %collective-permute-start.1 = (bf16[2,200,1024]{2,1,0:T(8,128)(2,1)}, bf16[2,200,1024]{2,1,0:T(8,128)(2,1)S(1)}, u32[]{:S(2)}, u32[]{:S(2)}) collective-permute-start(bf16[2,200,1024]{2,1,0:T(8,128)(2,1)} %bitcast.21), channel_id=1, source_target_pairs={{0,6},{1,7},{2,0},{3,1},{4,2},{5,3},{6,4},{7,5},{8,14},{9,15},{10,... | collective-permute-start | bytes 2457608 | tf_op jit(solution)/shard_map/ppermute | solution.py:29
  11.2 34.2 %collective-permute-start.2 = (bf16[2,200,1024]{2,1,0:T(8,128)(2,1)}, bf16[2,200,1024]{2,1,0:T(8,128)(2,1)}, u32[]{:S(2)}, u32[]{:S(2)}) collective-permute-start(bf16[2,200,1024]{2,1,0:T(8,128)(2,1)} %bitcast.22), channel_id=1, source_target_pairs={{0,1},{1,0},{2,3},{3,2},{4,5},{5,4},{6,7},{7,6},{8,9},{9,8},{10,11... | collective-permute-start | bytes 2457608 | tf_op jit(solution)/shard_map/ppermute | solution.py:29
  15.2 53.5 %copy-start.6 = (s32[4096]{0:T(1024)S(1)}, s32[4096]{0:T(1024)}, u32[]{:S(2)}) copy-start(s32[4096]{0:T(1024)} %index.3) | copy-start | bytes 49156
  29.5 44.2 %copy-start = (bf16[2,200,1024]{2,1,0:T(8,128)(2,1)}, bf16[2,200,1024]{2,1,0:T(8,128)(2,1)S(1)}, u32[]{:S(2)}) copy-start(bf16[2,200,1024]{2,1,0:T(8,128)(2,1)S(1)} %collective-permute-done.refs_1_) | copy-start | bytes 2457604
  29.5 44.2 %copy-start.1 = (bf16[2,200,1024]{2,1,0:T(8,128)(2,1)}, bf16[2,200,1024]{2,1,0:T(8,128)(2,1)S(1)}, u32[]{:S(2)}) copy-start(bf16[2,200,1024]{2,1,0:T(8,128)(2,1)S(1)} %collective-permute-done.1.refs_2_) | copy-start | bytes 2457604
  29.6 15.9 %collective-permute-start.3 = (bf16[1,200,1024]{2,1,0:T(8,128)(2,1)S(1)}, bf16[1,200,1024]{2,1,0:T(8,128)(2,1)S(1)}, u32[]{:S(2)}, u32[]{:S(2)}) collective-permute-start(bf16[1,200,1024]{2,1,0:T(8,128)(2,1)S(1)} %slice.18), channel_id=1, source_target_pairs={{0,2},{1,3},{2,4},{3,5},{4,6},{5,7},{6,0},{7,1},{8,10},{9,11},{10,... | collective-permute-start | bytes 1228808 | tf_op jit(solution)/shard_map/ppermute | solution.py:29
  31.3 14.2 %collective-permute-start.4 = (bf16[1,200,1024]{2,1,0:T(8,128)(2,1)S(1)}, bf16[1,200,1024]{2,1,0:T(8,128)(2,1)S(1)}, u32[]{:S(2)}, u32[]{:S(2)}) collective-permute-start(bf16[1,200,1024]{2,1,0:T(8,128)(2,1)S(1)} %slice.19), channel_id=1, source_target_pairs={{0,6},{1,7},{2,0},{3,1},{4,2},{5,3},{6,4},{7,5},{8,14},{9,15},{10,... | collective-permute-start | bytes 1228808 | tf_op jit(solution)/shard_map/ppermute | solution.py:29
  45.4 17.6 %copy-start.4 = (bf16[1,200,1024]{2,1,0:T(8,128)(2,1)}, bf16[1,200,1024]{2,1,0:T(8,128)(2,1)S(1)}, u32[]{:S(2)}) copy-start(bf16[1,200,1024]{2,1,0:T(8,128)(2,1)S(1)} %collective-permute-done.3.refs_3_) | copy-start | bytes 1228804
  45.4 17.6 %copy-start.5 = (bf16[1,200,1024]{2,1,0:T(8,128)(2,1)}, bf16[1,200,1024]{2,1,0:T(8,128)(2,1)S(1)}, u32[]{:S(2)}) copy-start(bf16[1,200,1024]{2,1,0:T(8,128)(2,1)S(1)} %collective-permute-done.4.refs_4_) | copy-start | bytes 1228804
  45.4 17.6 %collective-permute-start.5 = (bf16[2,200,1024]{2,1,0:T(8,128)(2,1)}, bf16[2,200,1024]{2,1,0:T(8,128)(2,1)S(1)}, u32[]{:S(2)}, u32[]{:S(2)}) collective-permute-start(bf16[2,200,1024]{2,1,0:T(8,128)(2,1)} %collective-permute-done.2.refs_5_), channel_id=1, source_target_pairs={{0,2},{1,3},{2,4},{3,5},{4,6},{5,7},{6,0},{7,1},{8,10},{9,11},{10,... | collective-permute-start | bytes 2457608 | tf_op jit(solution)/shard_map/ppermute | solution.py:29
  45.5 17.5 %collective-permute-start.6 = (bf16[2,200,1024]{2,1,0:T(8,128)(2,1)}, bf16[2,200,1024]{2,1,0:T(8,128)(2,1)S(1)}, u32[]{:S(2)}, u32[]{:S(2)}) collective-permute-start(bf16[2,200,1024]{2,1,0:T(8,128)(2,1)} %collective-permute-done.2.refs_5_), channel_id=1, source_target_pairs={{0,6},{1,7},{2,0},{3,1},{4,2},{5,3},{6,4},{7,5},{8,14},{9,15},{10,... | collective-permute-start | bytes 2457608 | tf_op jit(solution)/shard_map/ppermute | solution.py:29
  63.0 10.7 %copy-start.2 = (bf16[2,200,1024]{2,1,0:T(8,128)(2,1)}, bf16[2,200,1024]{2,1,0:T(8,128)(2,1)S(1)}, u32[]{:S(2)}) copy-start(bf16[2,200,1024]{2,1,0:T(8,128)(2,1)S(1)} %collective-permute-done.5.refs_6_) | copy-start | bytes 2457604
  63.1 10.7 %copy-start.3 = (bf16[2,200,1024]{2,1,0:T(8,128)(2,1)}, bf16[2,200,1024]{2,1,0:T(8,128)(2,1)S(1)}, u32[]{:S(2)}) copy-start(bf16[2,200,1024]{2,1,0:T(8,128)(2,1)S(1)} %collective-permute-done.6.refs_7_) | copy-start | bytes 2457604
  63.9 9.5 %collective-permute-start.7 = (bf16[1,200,1024]{2,1,0:T(8,128)(2,1)}, bf16[1,200,1024]{2,1,0:T(8,128)(2,1)}, u32[]{:S(2)}, u32[]{:S(2)}) collective-permute-start(bf16[1,200,1024]{2,1,0:T(8,128)(2,1)} %slice.20), channel_id=1, source_target_pairs={{0,2},{1,3},{2,4},{3,5},{4,6},{5,7},{6,0},{7,1},{8,10},{9,11},{10,... | collective-permute-start | bytes 1228808 | tf_op jit(solution)/shard_map/ppermute | solution.py:29
  64.7 9.0 %collective-permute-start.8 = (bf16[1,200,1024]{2,1,0:T(8,128)(2,1)}, bf16[1,200,1024]{2,1,0:T(8,128)(2,1)}, u32[]{:S(2)}, u32[]{:S(2)}) collective-permute-start(bf16[1,200,1024]{2,1,0:T(8,128)(2,1)} %slice.21), channel_id=1, source_target_pairs={{0,6},{1,7},{2,0},{3,1},{4,2},{5,3},{6,4},{7,5},{8,14},{9,15},{10,... | collective-permute-start | bytes 1228808 | tf_op jit(solution)/shard_map/ppermute | solution.py:29
  131.0 3.0 %collective-permute-start.9 = (f32[512,512]{1,0:T(8,128)}, f32[512,512]{1,0:T(8,128)S(1)}, u32[]{:S(2)}, u32[]{:S(2)}) collective-permute-start(f32[512,512]{1,0:T(8,128)} %get-tuple-element.23), channel_id=1, source_target_pairs={{0,8},{1,9},{2,10},{3,11},{4,12},{5,13},{6,14},{7,15},{8,0},{9,1},... | collective-permute-start | bytes 3145736 | tf_op jit(solution)/shard_map/ppermute | solution.py:256
Sparse Core Ops, SparseCore 0:
  9.7 87.4 all-gather.2

commit v5 on v4

--- a/solution.py
+++ b/solution.py
@@ -121,7 +121,7 @@
     )(index, order, *[piece for piece, _, _ in pieces])
 
 
-AHEAD = 3
+AHEAD = 6
 BLOCK = 256
 CHUNK = 16
 

time: 169 us -> 168 us (level)
  no operation moved by 1% of the time
where the time goes in v5:
time: 168 us
  Pallas kernels  62.5 us (37%)
  waiting for transfers between devices  42.7 us (25%)
  blocking collectives  25.8 us (15%)
  starting transfers between devices  17.5 us (10%)
  between operations  14.1 us (8%)
  other arithmetic  2.75 us (2%)
  local copies, waits for them, and re-layouts  2.39 us (1%)
    pallas_call x1, Pallas kernels, score_groups(): pl.pallas_call(group_kernel, out_shape=(jax.ShapeDtypeStruct((STEPS, 1, G...  32.8 us
    ppermute x9, waiting for transfers between devices, hop(): return lax.ppermute(array, BOTH, pairs)  32 us
    pallas_call x2, Pallas kernels, gather_rows(): pl.pallas_call(functools.partial(gather_kernel, places), out_shape=jax.Sh...  29.7 us
    all_to_all x1, blocking collectives, sum_at_owner(): lax.all_to_all(half.reshape(64, 8, WIDE), BOTH, 0, 0, axis_index_groups=g...  25.8 us
    ppermute x9, starting transfers between devices, hop(): return lax.ppermute(array, BOTH, pairs)  17.2 us
    all_gather x1, waiting for transfers between devices, body(): target = lax.all_gather(own, 'row', axis=0)  7.36 us
  transfers between devices with their start and end apart: 11, of which 7 were waited for; matrix products, arithmetic and copies ran while one was open for 2% of the time, Pallas kernels for 18%

profile of v5, /device:TPU:0, one launch (start us, length us, event | category | flops | bytes accessed | tf_op | source)
XLA Modules:
  0.0 167.7 jit_solution(14738444899441506524)
XLA Ops:
  7.2 0.7 all-gather.3.cloned.1.call-update
  7.9 1.7 %collective-permute-start = (bf16[2,200,1024]{2,1,0:T(8,128)(2,1)}, bf16[2,200,1024]{2,1,0:T(8,128)(2,1)S(1)}, u32[]{:S(2)}, u32[]{:S(2)}) collective-permute-start(bf16[2,200,1024]{2,1,0:T(8,128)(2,1)} %bitcast.20), channel_id=1, source_target_pairs={{0,2},{1,3},{2,4},{3,5},{4,6},{5,7},{6,0},{7,1},{8,10},{9,11},{10,... | collective-permute-start | bytes 2457608 | tf_op jit(solution)/shard_map/ppermute | solution.py:29
  9.6 1.6 collective-permute-start.1
  11.2 4.0 %collective-permute-start.2 = (bf16[2,200,1024]{2,1,0:T(8,128)(2,1)}, bf16[2,200,1024]{2,1,0:T(8,128)(2,1)}, u32[]{:S(2)}, u32[]{:S(2)}) collective-permute-start(bf16[2,200,1024]{2,1,0:T(8,128)(2,1)} %bitcast.22), channel_id=1, source_target_pairs={{0,1},{1,0},{2,3},{3,2},{4,5},{5,4},{6,7},{7,6},{8,9},{9,8},{10,11... | collective-permute-start | bytes 2457608 | tf_op jit(solution)/shard_map/ppermute | solution.py:29
  15.2 13.6 %gather_rows.2.rel = bf16[4096,512]{1,0:T(8,128)(2,1)} custom-call(s32[4096]{0:T(1024)} %index.3, s32[1]{0:T(128)} %constant.75.clone.1.order, bf16[2,200,1024]{2,1,0:T(8,128)(2,1)} %bitcast.24), custom_call_target="tpu_custom_call" | custom-call | bytes 28000000 | tf_op jit(solution)/shard_map/gather_rows/pallas_call | solution.py:103
  28.8 0.7 collective-permute-done.refs_1_
  29.6 1.6 collective-permute-start.3
  31.3 1.7 %collective-permute-start.4 = (bf16[1,200,1024]{2,1,0:T(8,128)(2,1)S(1)}, bf16[1,200,1024]{2,1,0:T(8,128)(2,1)S(1)}, u32[]{:S(2)}, u32[]{:S(2)}) collective-permute-start(bf16[1,200,1024]{2,1,0:T(8,128)(2,1)S(1)} %slice.19), channel_id=1, source_target_pairs={{0,6},{1,7},{2,0},{3,1},{4,2},{5,3},{6,4},{7,5},{8,14},{9,15},{10,... | collective-permute-start | bytes 1228808 | tf_op jit(solution)/shard_map/ppermute | solution.py:29
  33.0 12.4 %collective-permute-done.2.refs_5_ = bf16[2,200,1024]{2,1,0:T(8,128)(2,1)} collective-permute-done((bf16[2,200,1024]{2,1,0:T(8,128)(2,1)}, bf16[2,200,1024]{2,1,0:T(8,128)(2,1)}, u32[]{:S(2)}, u32[]{:S(2)}) %collective-permute-start.2) | collective-permute-done | bytes 819232 | tf_op jit(solution)/shard_map/ppermute | solution.py:29
  45.5 3.2 %collective-permute-start.6 = (bf16[2,200,1024]{2,1,0:T(8,128)(2,1)}, bf16[2,200,1024]{2,1,0:T(8,128)(2,1)S(1)}, u32[]{:S(2)}, u32[]{:S(2)}) collective-permute-start(bf16[2,200,1024]{2,1,0:T(8,128)(2,1)} %collective-permute-done.2.refs_5_), channel_id=1, source_target_pairs={{0,6},{1,7},{2,0},{3,1},{4,2},{5,3},{6,4},{7,5},{8,14},{9,15},{10,... | collective-permute-start | bytes 2457608 | tf_op jit(solution)/shard_map/ppermute | solution.py:29
  48.8 14.3 %collective-permute-done.5.refs_6_ = bf16[2,200,1024]{2,1,0:T(8,128)(2,1)S(1)} collective-permute-done((bf16[2,200,1024]{2,1,0:T(8,128)(2,1)}, bf16[2,200,1024]{2,1,0:T(8,128)(2,1)S(1)}, u32[]{:S(2)}, u32[]{:S(2)}) %collective-permute-start.5) | collective-permute-done | bytes 819232 | tf_op jit(solution)/shard_map/ppermute | solution.py:29
  63.1 0.9 slice.20
  63.9 0.8 slice.21
  64.7 3.2 %collective-permute-start.8 = (bf16[1,200,1024]{2,1,0:T(8,128)(2,1)}, bf16[1,200,1024]{2,1,0:T(8,128)(2,1)}, u32[]{:S(2)}, u32[]{:S(2)}) collective-permute-start(bf16[1,200,1024]{2,1,0:T(8,128)(2,1)} %slice.21), channel_id=1, source_target_pairs={{0,6},{1,7},{2,0},{3,1},{4,2},{5,3},{6,4},{7,5},{8,14},{9,15},{10,... | collective-permute-start | bytes 1228808 | tf_op jit(solution)/shard_map/ppermute | solution.py:29
  68.0 0.7 stack.44.order
  68.6 0.6 and_add_fusion
  69.2 4.2 %collective-permute-done.7.refs_8_ = bf16[1,200,1024]{2,1,0:T(8,128)(2,1)} collective-permute-done((bf16[1,200,1024]{2,1,0:T(8,128)(2,1)}, bf16[1,200,1024]{2,1,0:T(8,128)(2,1)}, u32[]{:S(2)}, u32[]{:S(2)}) %collective-permute-start.7) | collective-permute-done | bytes 409632 | tf_op jit(solution)/shard_map/ppermute | solution.py:29
  73.8 16.1 %gather_rows.3.src = bf16[4096,512]{1,0:T(8,128)(2,1)} custom-call(s32[4096]{0:T(1024)} %index.4, s32[8]{0:T(128)} %stack.44.order, bf16[2,200,1024]{2,1,0:T(8,128)(2,1)} %bitcast.23, bf16[2,200,1024]{2,1,0:T(8,128)(2,1)} %copy-done, bf16[2,200,1024]{2,1,0:T(8,128)(2,1)} %copy-done.1, bf16[1,200,1024]{2,1,0:T(8,128)(2,1)} %copy-done.4, ...), custom_call_target="tpu_custom_call" | custom-call | bytes 84000000 | tf_op jit(solution)/shard_map/gather_rows/pallas_call | solution.py:103
  89.8 7.4 %all-gather.3.cloned.1.call-done = bf16[32,200,1024]{2,1,0:T(8,128)(2,1)} async-done(((bf16[2,200,1024]{2,1,0:T(8,128)(2,1)}), bf16[32,200,1024]{2,1,0:T(8,128)(2,1)}) %all-gather.3.cloned.1.call-update) | async-done | bytes 13107216 | tf_op jit(solution)/shard_map/all_gather | solution.py:264
  97.2 32.8 %score_groups.1 = (f32[8,1,512]{2,1,0:T(1,128)}, f32[512,512]{1,0:T(8,128)}, f32[512,512]{1,0:T(8,128)}) custom-call(s32[4096]{0:T(1024)} %index.5, s32[8]{0:T(128)} %blocks.1, bf16[16,2,200,1024]{3,2,1,0:T(8,128)(2,1)} %bitcast.26, bf16[4096,512]{1,0:T(8,128)(2,1)} %gather_rows.3.src, bf16[4096,512]{1,0:T(8,128)(2,1)} %gather_rows.2.rel, s32[8,1,512]{2,1,0:T(1,128)} %bitcast.25), custom_call_target="tpu_custom_call" | custom-call | flops 20000000000 | bytes 24000000 | tf_op jit(solution)/shard_map/score_groups/pallas_call | solution.py:215
  130.3 2.6 %collective-permute-done.9 = f32[512,512]{1,0:T(8,128)S(1)} collective-permute-done((f32[512,512]{1,0:T(8,128)}, f32[512,512]{1,0:T(8,128)S(1)}, u32[]{:S(2)}, u32[]{:S(2)}) %collective-permute-start.9) | collective-permute-done | bytes 1048608 | tf_op jit(solution)/shard_map/ppermute | solution.py:256
  132.9 1.4 add_bitcast_fusion
  134.4 25.8 %all_to_all.5 = f32[64,8,512]{2,1,0:T(8,128)S(1)} all-to-all(f32[64,8,512]{2,1,0:T(8,128)S(1)} %add_bitcast_fusion), channel_id=1, replica_groups={{0,1,2,3,4,5,6,7,16,17,18,19,20,21,22,23,32,33,34,35,36,37,38,39,48,49,..., dimensions={0} | all-to-all | bytes 2097152 | tf_op jit(solution)/shard_map/all_to_all | solution.py:258
  160.3 0.6 pad_maximum_fusion
  (27 shorter events, 1.0 us)
Async XLA Ops:
  7.2 90.0 %all-gather.3.cloned.1.call-start = ((), (), s32[]{:S(2)}) async-start(), calls=%async_computation.1 | async-start | bytes 13926400 | tf_op jit(solution)/shard_map/all_gather | solution.py:264
  7.9 21.6 %collective-permute-start = (bf16[2,200,1024]{2,1,0:T(8,128)(2,1)}, bf16[2,200,1024]{2,1,0:T(8,128)(2,1)S(1)}, u32[]{:S(2)}, u32[]{:S(2)}) collective-permute-start(bf16[2,200,1024]{2,1,0:T(8,128)(2,1)} %bitcast.20), channel_id=1, source_target_pairs={{0,2},{1,3},{2,4},{3,5},{4,6},{5,7},{6,0},{7,1},{8,10},{9,11},{10,... | collective-permute-start | bytes 2457608 | tf_op jit(solution)/shard_map/ppermute | solution.py:29
  9.6 19.9 %collective-permute-start.1 = (bf16[2,200,1024]{2,1,0:T(8,128)(2,1)}, bf16[2,200,1024]{2,1,0:T(8,128)(2,1)S(1)}, u32[]{:S(2)}, u32[]{:S(2)}) collective-permute-start(bf16[2,200,1024]{2,1,0:T(8,128)(2,1)} %bitcast.21), channel_id=1, source_target_pairs={{0,6},{1,7},{2,0},{3,1},{4,2},{5,3},{6,4},{7,5},{8,14},{9,15},{10,... | collective-permute-start | bytes 2457608 | tf_op jit(solution)/shard_map/ppermute | solution.py:29
  11.2 34.2 %collective-permute-start.2 = (bf16[2,200,1024]{2,1,0:T(8,128)(2,1)}, bf16[2,200,1024]{2,1,0:T(8,128)(2,1)}, u32[]{:S(2)}, u32[]{:S(2)}) collective-permute-start(bf16[2,200,1024]{2,1,0:T(8,128)(2,1)} %bitcast.22), channel_id=1, source_target_pairs={{0,1},{1,0},{2,3},{3,2},{4,5},{5,4},{6,7},{7,6},{8,9},{9,8},{10,11... | collective-permute-start | bytes 2457608 | tf_op jit(solution)/shard_map/ppermute | solution.py:29
  15.2 53.5 %copy-start.6 = (s32[4096]{0:T(1024)S(1)}, s32[4096]{0:T(1024)}, u32[]{:S(2)}) copy-start(s32[4096]{0:T(1024)} %index.3) | copy-start | bytes 49156
  29.5 44.2 %copy-start = (bf16[2,200,1024]{2,1,0:T(8,128)(2,1)}, bf16[2,200,1024]{2,1,0:T(8,128)(2,1)S(1)}, u32[]{:S(2)}) copy-start(bf16[2,200,1024]{2,1,0:T(8,128)(2,1)S(1)} %collective-permute-done.refs_1_) | copy-start | bytes 2457604
  29.5 44.2 %copy-start.1 = (bf16[2,200,1024]{2,1,0:T(8,128)(2,1)}, bf16[2,200,1024]{2,1,0:T(8,128)(2,1)S(1)}, u32[]{:S(2)}) copy-start(bf16[2,200,1024]{2,1,0:T(8,128)(2,1)S(1)} %collective-permute-done.1.refs_2_) | copy-start | bytes 2457604
  29.6 15.9 %collective-permute-start.3 = (bf16[1,200,1024]{2,1,0:T(8,128)(2,1)S(1)}, bf16[1,200,1024]{2,1,0:T(8,128)(2,1)S(1)}, u32[]{:S(2)}, u32[]{:S(2)}) collective-permute-start(bf16[1,200,1024]{2,1,0:T(8,128)(2,1)S(1)} %slice.18), channel_id=1, source_target_pairs={{0,2},{1,3},{2,4},{3,5},{4,6},{5,7},{6,0},{7,1},{8,10},{9,11},{10,... | collective-permute-start | bytes 1228808 | tf_op jit(solution)/shard_map/ppermute | solution.py:29
  31.3 14.2 %collective-permute-start.4 = (bf16[1,200,1024]{2,1,0:T(8,128)(2,1)S(1)}, bf16[1,200,1024]{2,1,0:T(8,128)(2,1)S(1)}, u32[]{:S(2)}, u32[]{:S(2)}) collective-permute-start(bf16[1,200,1024]{2,1,0:T(8,128)(2,1)S(1)} %slice.19), channel_id=1, source_target_pairs={{0,6},{1,7},{2,0},{3,1},{4,2},{5,3},{6,4},{7,5},{8,14},{9,15},{10,... | collective-permute-start | bytes 1228808 | tf_op jit(solution)/shard_map/ppermute | solution.py:29
  45.4 17.6 %copy-start.4 = (bf16[1,200,1024]{2,1,0:T(8,128)(2,1)}, bf16[1,200,1024]{2,1,0:T(8,128)(2,1)S(1)}, u32[]{:S(2)}) copy-start(bf16[1,200,1024]{2,1,0:T(8,128)(2,1)S(1)} %collective-permute-done.3.refs_3_) | copy-start | bytes 1228804
  45.4 17.6 %copy-start.5 = (bf16[1,200,1024]{2,1,0:T(8,128)(2,1)}, bf16[1,200,1024]{2,1,0:T(8,128)(2,1)S(1)}, u32[]{:S(2)}) copy-start(bf16[1,200,1024]{2,1,0:T(8,128)(2,1)S(1)} %collective-permute-done.4.refs_4_) | copy-start | bytes 1228804
  45.4 17.6 %collective-permute-start.5 = (bf16[2,200,1024]{2,1,0:T(8,128)(2,1)}, bf16[2,200,1024]{2,1,0:T(8,128)(2,1)S(1)}, u32[]{:S(2)}, u32[]{:S(2)}) collective-permute-start(bf16[2,200,1024]{2,1,0:T(8,128)(2,1)} %collective-permute-done.2.refs_5_), channel_id=1, source_target_pairs={{0,2},{1,3},{2,4},{3,5},{4,6},{5,7},{6,0},{7,1},{8,10},{9,11},{10,... | collective-permute-start | bytes 2457608 | tf_op jit(solution)/shard_map/ppermute | solution.py:29
  45.5 17.5 %collective-permute-start.6 = (bf16[2,200,1024]{2,1,0:T(8,128)(2,1)}, bf16[2,200,1024]{2,1,0:T(8,128)(2,1)S(1)}, u32[]{:S(2)}, u32[]{:S(2)}) collective-permute-start(bf16[2,200,1024]{2,1,0:T(8,128)(2,1)} %collective-permute-done.2.refs_5_), channel_id=1, source_target_pairs={{0,6},{1,7},{2,0},{3,1},{4,2},{5,3},{6,4},{7,5},{8,14},{9,15},{10,... | collective-permute-start | bytes 2457608 | tf_op jit(solution)/shard_map/ppermute | solution.py:29
  63.0 10.7 %copy-start.2 = (bf16[2,200,1024]{2,1,0:T(8,128)(2,1)}, bf16[2,200,1024]{2,1,0:T(8,128)(2,1)S(1)}, u32[]{:S(2)}) copy-start(bf16[2,200,1024]{2,1,0:T(8,128)(2,1)S(1)} %collective-permute-done.5.refs_6_) | copy-start | bytes 2457604
  63.1 10.7 %copy-start.3 = (bf16[2,200,1024]{2,1,0:T(8,128)(2,1)}, bf16[2,200,1024]{2,1,0:T(8,128)(2,1)S(1)}, u32[]{:S(2)}) copy-start(bf16[2,200,1024]{2,1,0:T(8,128)(2,1)S(1)} %collective-permute-done.6.refs_7_) | copy-start | bytes 2457604
  63.9 9.5 %collective-permute-start.7 = (bf16[1,200,1024]{2,1,0:T(8,128)(2,1)}, bf16[1,200,1024]{2,1,0:T(8,128)(2,1)}, u32[]{:S(2)}, u32[]{:S(2)}) collective-permute-start(bf16[1,200,1024]{2,1,0:T(8,128)(2,1)} %slice.20), channel_id=1, source_target_pairs={{0,2},{1,3},{2,4},{3,5},{4,6},{5,7},{6,0},{7,1},{8,10},{9,11},{10,... | collective-permute-start | bytes 1228808 | tf_op jit(solution)/shard_map/ppermute | solution.py:29
  64.7 9.0 %collective-permute-start.8 = (bf16[1,200,1024]{2,1,0:T(8,128)(2,1)}, bf16[1,200,1024]{2,1,0:T(8,128)(2,1)}, u32[]{:S(2)}, u32[]{:S(2)}) collective-permute-start(bf16[1,200,1024]{2,1,0:T(8,128)(2,1)} %slice.21), channel_id=1, source_target_pairs={{0,6},{1,7},{2,0},{3,1},{4,2},{5,3},{6,4},{7,5},{8,14},{9,15},{10,... | collective-permute-start | bytes 1228808 | tf_op jit(solution)/shard_map/ppermute | solution.py:29
  130.0 3.0 %collective-permute-start.9 = (f32[512,512]{1,0:T(8,128)}, f32[512,512]{1,0:T(8,128)S(1)}, u32[]{:S(2)}, u32[]{:S(2)}) collective-permute-start(f32[512,512]{1,0:T(8,128)} %get-tuple-element.23), channel_id=1, source_target_pairs={{0,8},{1,9},{2,10},{3,11},{4,12},{5,13},{6,14},{7,15},{8,0},{9,1},... | collective-permute-start | bytes 3145736 | tf_op jit(solution)/shard_map/ppermute | solution.py:256
Sparse Core Ops, SparseCore 0:
  9.7 87.4 all-gather.2

commit v6 on v5

--- a/solution.py
+++ b/solution.py
@@ -64,7 +64,7 @@
     lax.fori_loop(0, SHARD // 128, tile, 0, unroll=8)
 
 
-def pick_rows(index, first, table, rows, unroll=16):
+def pick_rows(index, first, table, rows, unroll=64):
     def step(i, carry):
         b = i * unroll
         values = [table[pl.ds(index[first + b + u], 1), :] for u in range(unroll)]
@@ -121,7 +121,7 @@
     )(index, order, *[piece for piece, _, _ in pieces])
 
 
-AHEAD = 6
+AHEAD = 16
 BLOCK = 256
 CHUNK = 16
 

time: 168 us -> 168 us (level)
  Pallas kernels: 62.5 us -> 60.4 us
  waiting for transfers between devices: 42.7 us -> 44.6 us
    pallas_call x2, Pallas kernels: 29.7 us -> 27.8 us  [gather_rows(): pl.pallas_call(functools.partial(gather_kernel, places), out_shape=jax.Sh...]
  transfers between devices with their start and end apart: 11 -> 11, of which waited for: 7 -> 7; matrix products, arithmetic and copies ran while one was open for 2% -> 2% of each run, Pallas kernels for 18% -> 17%
where the time goes in v6:
time: 168 us
  Pallas kernels  60.4 us (36%)
  waiting for transfers between devices  44.6 us (27%)
  blocking collectives  25.8 us (15%)
  starting transfers between devices  17.5 us (10%)
  between operations  14.1 us (8%)
  other arithmetic  2.75 us (2%)
  local copies, waits for them, and re-layouts  2.39 us (1%)
    ppermute x9, waiting for transfers between devices, hop(): return lax.ppermute(array, BOTH, pairs)  33 us
    pallas_call x1, Pallas kernels, score_groups(): pl.pallas_call(group_kernel, out_shape=(jax.ShapeDtypeStruct((STEPS, 1, G...  32.7 us
    pallas_call x2, Pallas kernels, gather_rows(): pl.pallas_call(functools.partial(gather_kernel, places), out_shape=jax.Sh...  27.8 us
    all_to_all x1, blocking collectives, sum_at_owner(): lax.all_to_all(half.reshape(64, 8, WIDE), BOTH, 0, 0, axis_index_groups=g...  25.8 us
    ppermute x9, starting transfers between devices, hop(): return lax.ppermute(array, BOTH, pairs)  17.2 us
    all_gather x1, waiting for transfers between devices, body(): target = lax.all_gather(own, 'row', axis=0)  8.33 us
  transfers between devices with their start and end apart: 11, of which 7 were waited for; matrix products, arithmetic and copies ran while one was open for 2% of the time, Pallas kernels for 17%

profile of v6, /device:TPU:0, one launch (start us, length us, event | category | flops | bytes accessed | tf_op | source)
XLA Modules:
  0.0 167.6 jit_solution(11410968180716297775)
XLA Ops:
  7.2 0.7 all-gather.3.cloned.1.call-update
  7.9 1.7 %collective-permute-start = (bf16[2,200,1024]{2,1,0:T(8,128)(2,1)}, bf16[2,200,1024]{2,1,0:T(8,128)(2,1)S(1)}, u32[]{:S(2)}, u32[]{:S(2)}) collective-permute-start(bf16[2,200,1024]{2,1,0:T(8,128)(2,1)} %bitcast.20), channel_id=1, source_target_pairs={{0,2},{1,3},{2,4},{3,5},{4,6},{5,7},{6,0},{7,1},{8,10},{9,11},{10,... | collective-permute-start | bytes 2457608 | tf_op jit(solution)/shard_map/ppermute | solution.py:29
  9.6 1.6 collective-permute-start.1
  11.2 4.0 %collective-permute-start.2 = (bf16[2,200,1024]{2,1,0:T(8,128)(2,1)}, bf16[2,200,1024]{2,1,0:T(8,128)(2,1)}, u32[]{:S(2)}, u32[]{:S(2)}) collective-permute-start(bf16[2,200,1024]{2,1,0:T(8,128)(2,1)} %bitcast.22), channel_id=1, source_target_pairs={{0,1},{1,0},{2,3},{3,2},{4,5},{5,4},{6,7},{7,6},{8,9},{9,8},{10,11... | collective-permute-start | bytes 2457608 | tf_op jit(solution)/shard_map/ppermute | solution.py:29
  15.2 12.7 %gather_rows.2.rel = bf16[4096,512]{1,0:T(8,128)(2,1)} custom-call(s32[4096]{0:T(1024)} %index.3, s32[1]{0:T(128)} %constant.75.clone.1.order, bf16[2,200,1024]{2,1,0:T(8,128)(2,1)} %bitcast.24), custom_call_target="tpu_custom_call" | custom-call | bytes 28000000 | tf_op jit(solution)/shard_map/gather_rows/pallas_call | solution.py:103
  27.8 1.7 %collective-permute-done.refs_1_ = bf16[2,200,1024]{2,1,0:T(8,128)(2,1)S(1)} collective-permute-done((bf16[2,200,1024]{2,1,0:T(8,128)(2,1)}, bf16[2,200,1024]{2,1,0:T(8,128)(2,1)S(1)}, u32[]{:S(2)}, u32[]{:S(2)}) %collective-permute-start) | collective-permute-done | bytes 819232 | tf_op jit(solution)/shard_map/ppermute | solution.py:29
  29.6 1.6 collective-permute-start.3
  31.3 1.7 %collective-permute-start.4 = (bf16[1,200,1024]{2,1,0:T(8,128)(2,1)S(1)}, bf16[1,200,1024]{2,1,0:T(8,128)(2,1)S(1)}, u32[]{:S(2)}, u32[]{:S(2)}) collective-permute-start(bf16[1,200,1024]{2,1,0:T(8,128)(2,1)S(1)} %slice.19), channel_id=1, source_target_pairs={{0,6},{1,7},{2,0},{3,1},{4,2},{5,3},{6,4},{7,5},{8,14},{9,15},{10,... | collective-permute-start | bytes 1228808 | tf_op jit(solution)/shard_map/ppermute | solution.py:29
  33.0 12.4 %collective-permute-done.2.refs_5_ = bf16[2,200,1024]{2,1,0:T(8,128)(2,1)} collective-permute-done((bf16[2,200,1024]{2,1,0:T(8,128)(2,1)}, bf16[2,200,1024]{2,1,0:T(8,128)(2,1)}, u32[]{:S(2)}, u32[]{:S(2)}) %collective-permute-start.2) | collective-permute-done | bytes 819232 | tf_op jit(solution)/shard_map/ppermute | solution.py:29
  45.5 3.2 %collective-permute-start.6 = (bf16[2,200,1024]{2,1,0:T(8,128)(2,1)}, bf16[2,200,1024]{2,1,0:T(8,128)(2,1)S(1)}, u32[]{:S(2)}, u32[]{:S(2)}) collective-permute-start(bf16[2,200,1024]{2,1,0:T(8,128)(2,1)} %collective-permute-done.2.refs_5_), channel_id=1, source_target_pairs={{0,6},{1,7},{2,0},{3,1},{4,2},{5,3},{6,4},{7,5},{8,14},{9,15},{10,... | collective-permute-start | bytes 2457608 | tf_op jit(solution)/shard_map/ppermute | solution.py:29
  48.8 14.3 %collective-permute-done.5.refs_6_ = bf16[2,200,1024]{2,1,0:T(8,128)(2,1)S(1)} collective-permute-done((bf16[2,200,1024]{2,1,0:T(8,128)(2,1)}, bf16[2,200,1024]{2,1,0:T(8,128)(2,1)S(1)}, u32[]{:S(2)}, u32[]{:S(2)}) %collective-permute-start.5) | collective-permute-done | bytes 819232 | tf_op jit(solution)/shard_map/ppermute | solution.py:29
  63.1 0.9 slice.20
  63.9 0.8 slice.21
  64.7 3.2 %collective-permute-start.8 = (bf16[1,200,1024]{2,1,0:T(8,128)(2,1)}, bf16[1,200,1024]{2,1,0:T(8,128)(2,1)}, u32[]{:S(2)}, u32[]{:S(2)}) collective-permute-start(bf16[1,200,1024]{2,1,0:T(8,128)(2,1)} %slice.21), channel_id=1, source_target_pairs={{0,6},{1,7},{2,0},{3,1},{4,2},{5,3},{6,4},{7,5},{8,14},{9,15},{10,... | collective-permute-start | bytes 1228808 | tf_op jit(solution)/shard_map/ppermute | solution.py:29
  68.0 0.7 stack.44.order
  68.6 0.6 and_add_fusion
  69.2 4.2 %collective-permute-done.7.refs_8_ = bf16[1,200,1024]{2,1,0:T(8,128)(2,1)} collective-permute-done((bf16[1,200,1024]{2,1,0:T(8,128)(2,1)}, bf16[1,200,1024]{2,1,0:T(8,128)(2,1)}, u32[]{:S(2)}, u32[]{:S(2)}) %collective-permute-start.7) | collective-permute-done | bytes 409632 | tf_op jit(solution)/shard_map/ppermute | solution.py:29
  73.8 15.1 %gather_rows.3.src = bf16[4096,512]{1,0:T(8,128)(2,1)} custom-call(s32[4096]{0:T(1024)} %index.4, s32[8]{0:T(128)} %stack.44.order, bf16[2,200,1024]{2,1,0:T(8,128)(2,1)} %bitcast.23, bf16[2,200,1024]{2,1,0:T(8,128)(2,1)} %copy-done, bf16[2,200,1024]{2,1,0:T(8,128)(2,1)} %copy-done.1, bf16[1,200,1024]{2,1,0:T(8,128)(2,1)} %copy-done.4, ...), custom_call_target="tpu_custom_call" | custom-call | bytes 84000000 | tf_op jit(solution)/shard_map/gather_rows/pallas_call | solution.py:103
  88.9 8.3 %all-gather.3.cloned.1.call-done = bf16[32,200,1024]{2,1,0:T(8,128)(2,1)} async-done(((bf16[2,200,1024]{2,1,0:T(8,128)(2,1)}), bf16[32,200,1024]{2,1,0:T(8,128)(2,1)}) %all-gather.3.cloned.1.call-update) | async-done | bytes 13107216 | tf_op jit(solution)/shard_map/all_gather | solution.py:264
  97.2 32.7 %score_groups.1 = (f32[8,1,512]{2,1,0:T(1,128)}, f32[512,512]{1,0:T(8,128)}, f32[512,512]{1,0:T(8,128)}) custom-call(s32[4096]{0:T(1024)} %index.5, s32[8]{0:T(128)} %blocks.1, bf16[16,2,200,1024]{3,2,1,0:T(8,128)(2,1)} %bitcast.26, bf16[4096,512]{1,0:T(8,128)(2,1)} %gather_rows.3.src, bf16[4096,512]{1,0:T(8,128)(2,1)} %gather_rows.2.rel, s32[8,1,512]{2,1,0:T(1,128)} %bitcast.25), custom_call_target="tpu_custom_call" | custom-call | flops 20000000000 | bytes 24000000 | tf_op jit(solution)/shard_map/score_groups/pallas_call | solution.py:215
  130.2 2.6 %collective-permute-done.9 = f32[512,512]{1,0:T(8,128)S(1)} collective-permute-done((f32[512,512]{1,0:T(8,128)}, f32[512,512]{1,0:T(8,128)S(1)}, u32[]{:S(2)}, u32[]{:S(2)}) %collective-permute-start.9) | collective-permute-done | bytes 1048608 | tf_op jit(solution)/shard_map/ppermute | solution.py:256
  132.8 1.4 add_bitcast_fusion
  134.3 25.8 %all_to_all.5 = f32[64,8,512]{2,1,0:T(8,128)S(1)} all-to-all(f32[64,8,512]{2,1,0:T(8,128)S(1)} %add_bitcast_fusion), channel_id=1, replica_groups={{0,1,2,3,4,5,6,7,16,17,18,19,20,21,22,23,32,33,34,35,36,37,38,39,48,49,..., dimensions={0} | all-to-all | bytes 2097152 | tf_op jit(solution)/shard_map/all_to_all | solution.py:258
  160.2 0.6 pad_maximum_fusion
  (27 shorter events, 1.0 us)
Async XLA Ops:
  7.2 90.0 %all-gather.3.cloned.1.call-start = ((), (), s32[]{:S(2)}) async-start(), calls=%async_computation.1 | async-start | bytes 13926400 | tf_op jit(solution)/shard_map/all_gather | solution.py:264
  7.9 21.6 %collective-permute-start = (bf16[2,200,1024]{2,1,0:T(8,128)(2,1)}, bf16[2,200,1024]{2,1,0:T(8,128)(2,1)S(1)}, u32[]{:S(2)}, u32[]{:S(2)}) collective-permute-start(bf16[2,200,1024]{2,1,0:T(8,128)(2,1)} %bitcast.20), channel_id=1, source_target_pairs={{0,2},{1,3},{2,4},{3,5},{4,6},{5,7},{6,0},{7,1},{8,10},{9,11},{10,... | collective-permute-start | bytes 2457608 | tf_op jit(solution)/shard_map/ppermute | solution.py:29
  9.6 19.9 %collective-permute-start.1 = (bf16[2,200,1024]{2,1,0:T(8,128)(2,1)}, bf16[2,200,1024]{2,1,0:T(8,128)(2,1)S(1)}, u32[]{:S(2)}, u32[]{:S(2)}) collective-permute-start(bf16[2,200,1024]{2,1,0:T(8,128)(2,1)} %bitcast.21), channel_id=1, source_target_pairs={{0,6},{1,7},{2,0},{3,1},{4,2},{5,3},{6,4},{7,5},{8,14},{9,15},{10,... | collective-permute-start | bytes 2457608 | tf_op jit(solution)/shard_map/ppermute | solution.py:29
  11.2 34.2 %collective-permute-start.2 = (bf16[2,200,1024]{2,1,0:T(8,128)(2,1)}, bf16[2,200,1024]{2,1,0:T(8,128)(2,1)}, u32[]{:S(2)}, u32[]{:S(2)}) collective-permute-start(bf16[2,200,1024]{2,1,0:T(8,128)(2,1)} %bitcast.22), channel_id=1, source_target_pairs={{0,1},{1,0},{2,3},{3,2},{4,5},{5,4},{6,7},{7,6},{8,9},{9,8},{10,11... | collective-permute-start | bytes 2457608 | tf_op jit(solution)/shard_map/ppermute | solution.py:29
  15.2 53.5 %copy-start.6 = (s32[4096]{0:T(1024)S(1)}, s32[4096]{0:T(1024)}, u32[]{:S(2)}) copy-start(s32[4096]{0:T(1024)} %index.3) | copy-start | bytes 49156
  29.5 44.2 %copy-start = (bf16[2,200,1024]{2,1,0:T(8,128)(2,1)}, bf16[2,200,1024]{2,1,0:T(8,128)(2,1)S(1)}, u32[]{:S(2)}) copy-start(bf16[2,200,1024]{2,1,0:T(8,128)(2,1)S(1)} %collective-permute-done.refs_1_) | copy-start | bytes 2457604
  29.5 44.2 %copy-start.1 = (bf16[2,200,1024]{2,1,0:T(8,128)(2,1)}, bf16[2,200,1024]{2,1,0:T(8,128)(2,1)S(1)}, u32[]{:S(2)}) copy-start(bf16[2,200,1024]{2,1,0:T(8,128)(2,1)S(1)} %collective-permute-done.1.refs_2_) | copy-start | bytes 2457604
  29.6 15.9 %collective-permute-start.3 = (bf16[1,200,1024]{2,1,0:T(8,128)(2,1)S(1)}, bf16[1,200,1024]{2,1,0:T(8,128)(2,1)S(1)}, u32[]{:S(2)}, u32[]{:S(2)}) collective-permute-start(bf16[1,200,1024]{2,1,0:T(8,128)(2,1)S(1)} %slice.18), channel_id=1, source_target_pairs={{0,2},{1,3},{2,4},{3,5},{4,6},{5,7},{6,0},{7,1},{8,10},{9,11},{10,... | collective-permute-start | bytes 1228808 | tf_op jit(solution)/shard_map/ppermute | solution.py:29
  31.3 14.2 %collective-permute-start.4 = (bf16[1,200,1024]{2,1,0:T(8,128)(2,1)S(1)}, bf16[1,200,1024]{2,1,0:T(8,128)(2,1)S(1)}, u32[]{:S(2)}, u32[]{:S(2)}) collective-permute-start(bf16[1,200,1024]{2,1,0:T(8,128)(2,1)S(1)} %slice.19), channel_id=1, source_target_pairs={{0,6},{1,7},{2,0},{3,1},{4,2},{5,3},{6,4},{7,5},{8,14},{9,15},{10,... | collective-permute-start | bytes 1228808 | tf_op jit(solution)/shard_map/ppermute | solution.py:29
  45.4 17.6 %copy-start.4 = (bf16[1,200,1024]{2,1,0:T(8,128)(2,1)}, bf16[1,200,1024]{2,1,0:T(8,128)(2,1)S(1)}, u32[]{:S(2)}) copy-start(bf16[1,200,1024]{2,1,0:T(8,128)(2,1)S(1)} %collective-permute-done.3.refs_3_) | copy-start | bytes 1228804
  45.4 17.6 %copy-start.5 = (bf16[1,200,1024]{2,1,0:T(8,128)(2,1)}, bf16[1,200,1024]{2,1,0:T(8,128)(2,1)S(1)}, u32[]{:S(2)}) copy-start(bf16[1,200,1024]{2,1,0:T(8,128)(2,1)S(1)} %collective-permute-done.4.refs_4_) | copy-start | bytes 1228804
  45.4 17.6 %collective-permute-start.5 = (bf16[2,200,1024]{2,1,0:T(8,128)(2,1)}, bf16[2,200,1024]{2,1,0:T(8,128)(2,1)S(1)}, u32[]{:S(2)}, u32[]{:S(2)}) collective-permute-start(bf16[2,200,1024]{2,1,0:T(8,128)(2,1)} %collective-permute-done.2.refs_5_), channel_id=1, source_target_pairs={{0,2},{1,3},{2,4},{3,5},{4,6},{5,7},{6,0},{7,1},{8,10},{9,11},{10,... | collective-permute-start | bytes 2457608 | tf_op jit(solution)/shard_map/ppermute | solution.py:29
  45.5 17.5 %collective-permute-start.6 = (bf16[2,200,1024]{2,1,0:T(8,128)(2,1)}, bf16[2,200,1024]{2,1,0:T(8,128)(2,1)S(1)}, u32[]{:S(2)}, u32[]{:S(2)}) collective-permute-start(bf16[2,200,1024]{2,1,0:T(8,128)(2,1)} %collective-permute-done.2.refs_5_), channel_id=1, source_target_pairs={{0,6},{1,7},{2,0},{3,1},{4,2},{5,3},{6,4},{7,5},{8,14},{9,15},{10,... | collective-permute-start | bytes 2457608 | tf_op jit(solution)/shard_map/ppermute | solution.py:29
  63.0 10.7 %copy-start.2 = (bf16[2,200,1024]{2,1,0:T(8,128)(2,1)}, bf16[2,200,1024]{2,1,0:T(8,128)(2,1)S(1)}, u32[]{:S(2)}) copy-start(bf16[2,200,1024]{2,1,0:T(8,128)(2,1)S(1)} %collective-permute-done.5.refs_6_) | copy-start | bytes 2457604
  63.1 10.7 %copy-start.3 = (bf16[2,200,1024]{2,1,0:T(8,128)(2,1)}, bf16[2,200,1024]{2,1,0:T(8,128)(2,1)S(1)}, u32[]{:S(2)}) copy-start(bf16[2,200,1024]{2,1,0:T(8,128)(2,1)S(1)} %collective-permute-done.6.refs_7_) | copy-start | bytes 2457604
  63.9 9.5 %collective-permute-start.7 = (bf16[1,200,1024]{2,1,0:T(8,128)(2,1)}, bf16[1,200,1024]{2,1,0:T(8,128)(2,1)}, u32[]{:S(2)}, u32[]{:S(2)}) collective-permute-start(bf16[1,200,1024]{2,1,0:T(8,128)(2,1)} %slice.20), channel_id=1, source_target_pairs={{0,2},{1,3},{2,4},{3,5},{4,6},{5,7},{6,0},{7,1},{8,10},{9,11},{10,... | collective-permute-start | bytes 1228808 | tf_op jit(solution)/shard_map/ppermute | solution.py:29
  64.7 9.0 %collective-permute-start.8 = (bf16[1,200,1024]{2,1,0:T(8,128)(2,1)}, bf16[1,200,1024]{2,1,0:T(8,128)(2,1)}, u32[]{:S(2)}, u32[]{:S(2)}) collective-permute-start(bf16[1,200,1024]{2,1,0:T(8,128)(2,1)} %slice.21), channel_id=1, source_target_pairs={{0,6},{1,7},{2,0},{3,1},{4,2},{5,3},{6,4},{7,5},{8,14},{9,15},{10,... | collective-permute-start | bytes 1228808 | tf_op jit(solution)/shard_map/ppermute | solution.py:29
  129.9 3.0 %collective-permute-start.9 = (f32[512,512]{1,0:T(8,128)}, f32[512,512]{1,0:T(8,128)S(1)}, u32[]{:S(2)}, u32[]{:S(2)}) collective-permute-start(f32[512,512]{1,0:T(8,128)} %get-tuple-element.23), channel_id=1, source_target_pairs={{0,8},{1,9},{2,10},{3,11},{4,12},{5,13},{6,14},{7,15},{8,0},{9,1},... | collective-permute-start | bytes 3145736 | tf_op jit(solution)/shard_map/ppermute | solution.py:256
Sparse Core Ops, SparseCore 0:
  9.7 87.4 all-gather.2
